TPU v7x, 512 devices: a whole 4x4x16 slice. The times are simulated.
512 devices in a mesh: dom: 64 (over x, z), cell: 8 (over y, core).
Axes of the slice: x: 4, y: 4, z: 16, core: 2. Of those that a mesh axis runs over, the one named last changes fastest.
Arguments:
- features: bfloat16 [131072, 128], P(('cell', 'dom')), parts along dimension 0, may hold values from -6 to 6
- positions: float32 [3, 131072], P(None, ('cell', 'dom')), parts along dimension 1, may hold values from 0 to 320, as said below
- neighbours: int32 [131072, 64], P(('cell', 'dom')), parts along dimension 0, may hold values from 0 to 767, as said below
- neighbour_count: int32 [131072], P(('cell', 'dom')), parts along dimension 0, may hold values from 16 to 64, as said below
- ghost_sends: int32 [2, 131072], P(None, ('cell', 'dom')), parts along dimension 1, may hold values from 0 to 255, as said below
- species: int32 [131072], P(('cell', 'dom')), parts along dimension 0, may hold values from 0 to 5
- wave_index: int32 [3, 1024], replicated, may hold values from -8 to 8, as said below
- force_ref: float32 [3, 131072], P(None, ('cell', 'dom')), parts along dimension 1, may hold values from -6 to 6
- radial_weight: bfloat16 [16, 128], replicated, may hold values from -1.5 to 1.5
- mix_weight: bfloat16 [128, 128], replicated, may hold values from -0.5 to 0.5
- charge_weight: bfloat16 [128, 64], replicated, may hold values from -0.5 to 0.5
- species_charge: float32 [6, 64], replicated, may hold values from -4 to 4
Outputs:
- forces: float32 [3, 131072], P(None, ('cell', 'dom')), parts along dimension 1
- radial_step: float32 [128, 128], P('cell'), parts along dimension 0
- mix_step: float32 [1024, 128], P('cell'), parts along dimension 0
- charge_step: float32 [1024, 64], P('cell'), parts along dimension 0
- species_step: float32 [48, 64], P('cell'), parts along dimension 0
There are 8 independent parts, one for each index of `cell`. A program takes and returns all parts, laid end to end along the dimension named above; an argument that names none is the same for every part. Nothing has to cross between parts.
Inputs may be any that keep to these rules, and one draw needn't show every extreme that they name: `neighbours`: in the shard of domain d, an entry e below 256 names the domain's own atom e; 256 + g names the atom at position g of row 1 of ghost_sends of domain d - 1; 512 + g names the atom at position g of row 0 of ghost_sends of domain d + 1 (domains cyclic). Entries of a row are distinct and never the atom itself. `neighbour_count`: slots below the count are live; in every domain some atom has all 64 slots live. `ghost_sends`: positions within the domain's shard; the entries of one row of one domain are distinct. `wave_index`: columns are distinct and their first component is 1 or more. `positions`: coordinates in a periodic box of 320 along the first axis and 20 along the other two.
All inputs are finite; a program needn't handle non-finite values.
Results may differ from a plain program's by a relative error of at most 0.0051.
Values may be sent and summed in bfloat16 or wider, within the bound.
A program may use at most 64 MiB of HBM per device.

v0:
```python
import jax
import jax.numpy as jnp
from jax import lax
from jax.sharding import PartitionSpec as P

cutoff_radius = 5.0
kernel_width = 1.0
basis_width = 0.5
box_side = 20.0
two_pi = 6.283185307179586
highest = lax.Precision.HIGHEST


def extended(shard, sides, width):
    for axis, dim in sides:
        devices, length = (lax.axis_size(axis), shard.shape[dim])
        up = [(i, (i + 1) % devices) for i in range(devices)]
        down = [(j, i) for i, j in up]
        last = lax.slice_in_dim(shard, length - width, length, axis=dim)
        initial = lax.slice_in_dim(shard, 0, width, axis=dim)
        before = lax.ppermute(last, axis, up)
        after = lax.ppermute(initial, axis, down)
        shard = jnp.concatenate([before, shard, after], axis=dim)
    return shard


def contract_first(left, right):
    return lax.dot_general(
        left, right, (((0,), (0,)), ((), ())), precision=highest, preferred_element_type=jnp.float32
    )


def contract_last(left, right):
    return lax.dot_general(
        left, right, (((1,), (1,)), ((), ())), precision=highest, preferred_element_type=jnp.float32
    )


def product(left, right):
    return jnp.dot(left, right, precision=highest, preferred_element_type=jnp.float32)


def edge_terms(own_coords, other_coords, live_count, box_lengths, basis_count):
    slots_count = other_coords.shape[2]
    displacement = other_coords - own_coords[:, :, None]
    displacement = displacement - box_lengths[:, None, None] * jnp.floor(
        displacement / box_lengths[:, None, None] + 0.5
    )
    distance = jnp.sqrt(jnp.sum(displacement * displacement, axis=0))
    is_live = (jnp.arange(slots_count, dtype=jnp.int32)[None, :] < live_count[:, None]).astype(
        jnp.float32
    )
    cutoff_fade = 0.5 * (
        jnp.cos(jnp.pi * jnp.minimum(distance, cutoff_radius) / cutoff_radius) + 1.0
    )
    centers = 0.5 + (cutoff_radius - 0.5) * jnp.arange(basis_count, dtype=jnp.float32) / (
        basis_count - 1
    )
    basis_rows = jnp.exp(-jnp.square((distance[..., None] - centers) / basis_width)).astype(
        jnp.bfloat16
    )
    return (basis_rows, is_live * cutoff_fade)


def silu_slope(value):
    sigmoid = jax.nn.sigmoid(value)
    return sigmoid * (1.0 + value * (1.0 - sigmoid))


def normalized(gradient):
    return gradient / jnp.sqrt(jnp.mean(gradient * gradient) + 1e-06)


def on_device(
    features,
    positions,
    neighbours,
    neighbour_count,
    ghost_sends,
    species,
    wave_index,
    force_ref,
    radial_weight,
    mix_weight,
    charge_weight,
    species_charge,
):
    atoms, width = features.shape
    slots_count = neighbours.shape[1]
    basis_count = radial_weight.shape[0]
    charges_width = charge_weight.shape[1]
    wave_count = wave_index.shape[1]
    domains = lax.axis_size("dom")
    total_atoms = atoms * domains
    box_lengths = jnp.array([1.25 * total_atoms / 64, box_side, box_side], dtype=jnp.float32)
    outgoing = features[ghost_sends]
    arrived = extended(outgoing, (("dom", 0),), 1)
    feature_table = jnp.concatenate([features, arrived[0], arrived[3]], axis=0)
    outgoing_coords = jnp.stack(
        [positions[:, ghost_sends[0]], positions[:, ghost_sends[1]]], axis=0
    )
    arrived_coords = extended(outgoing_coords, (("dom", 0),), 1)
    coords_all = jnp.concatenate([positions, arrived_coords[0], arrived_coords[3]], axis=1)
    edge_rows = 64
    blocks = atoms // edge_rows
    slot_blocks = neighbours.reshape(blocks, edge_rows, slots_count)
    own_blocks = positions.reshape(3, blocks, edge_rows).transpose(1, 0, 2)
    count_blocks = neighbour_count.reshape(blocks, edge_rows)

    def message_block(block_args):
        slot_rows, own_coords, live_count = block_args
        basis_rows, edge_weight = edge_terms(
            own_coords, coords_all[:, slot_rows], live_count, box_lengths, basis_count
        )
        filters = jnp.dot(
            basis_rows.reshape(-1, basis_count), radial_weight, preferred_element_type=jnp.float32
        )
        filters = filters.reshape(edge_rows, slots_count, width)
        return jnp.sum(
            edge_weight[..., None] * filters * feature_table[slot_rows].astype(jnp.float32), axis=1
        )

    messages = (
        lax.map(message_block, (slot_blocks, own_blocks, count_blocks))
        .reshape(atoms, width)
        .astype(jnp.bfloat16)
    )
    before = jnp.dot(messages, mix_weight, preferred_element_type=jnp.float32)
    hidden = (features.astype(jnp.float32) + jax.nn.silu(before)).astype(jnp.bfloat16)
    one_hot = (
        species[:, None] == jnp.arange(species_charge.shape[0], dtype=jnp.int32)[None, :]
    ).astype(jnp.float32)
    charges = jnp.dot(hidden, charge_weight, preferred_element_type=jnp.float32) + product(
        one_hot, species_charge
    )
    wave_vectors = two_pi * wave_index.astype(jnp.float32) / box_lengths[:, None]
    damping = (
        jnp.exp(-0.5 * kernel_width * kernel_width * jnp.sum(wave_vectors * wave_vectors, axis=0))
        / total_atoms
    )

    def phases_of(first_wave, wave_total):
        wave_piece = lax.dynamic_slice_in_dim(wave_vectors, first_wave, wave_total, 1)
        phases = contract_first(positions, wave_piece)
        return (jnp.cos(phases), jnp.sin(phases), wave_piece)

    def structure_term(first_wave, wave_total):
        cosines, sines, wave_piece = phases_of(first_wave, wave_total)
        return jnp.concatenate(
            [contract_first(cosines, charges), contract_first(sines, charges)], axis=1
        )

    def force_piece(running, coeff_piece, first_wave):
        cosines, sines, wave_piece = phases_of(first_wave, coeff_piece.shape[0])
        along_cos = contract_last(charges, coeff_piece[:, :charges_width])
        along_sin = contract_last(charges, coeff_piece[:, charges_width:])
        mixture = sines * along_cos - cosines * along_sin
        return running + contract_last(wave_piece, mixture)

    wave_rows = min(wave_count, 256)
    wave_blocks = wave_count // wave_rows
    first_waves = jnp.arange(wave_blocks, dtype=jnp.int32) * wave_rows

    def structure_block(first_wave):
        return structure_term(first_wave, wave_rows)

    wave_terms = lax.map(structure_block, first_waves).reshape(wave_count, 2 * charges_width)
    structure = lax.psum(wave_terms, "dom")
    coefficients = damping[:, None] * structure

    def force_step(running, first_wave):
        coeff_piece = lax.dynamic_slice_in_dim(coefficients, first_wave, wave_rows, 0)
        return (force_piece(running, coeff_piece, first_wave), None)

    forces, _ = lax.scan(force_step, jnp.zeros((3, atoms), jnp.float32), first_waves)
    errors = 2.0 * (forces - force_ref)

    def gradient_step(running, first_wave):
        cosines, sines, wave_piece = phases_of(first_wave, wave_rows)
        slopes = contract_first(errors, wave_piece)
        coeff_piece = lax.dynamic_slice_in_dim(coefficients, first_wave, wave_rows, 0)
        direct = product(slopes * sines, coeff_piece[:, :charges_width]) - product(
            slopes * cosines, coeff_piece[:, charges_width:]
        )
        wave_term = jnp.concatenate(
            [contract_first(slopes * sines, charges), -contract_first(slopes * cosines, charges)],
            axis=1,
        )
        return (running + direct, wave_term)

    direct_sum, gradient_terms = lax.scan(
        gradient_step, jnp.zeros((atoms, charges_width), jnp.float32), first_waves
    )
    gradient_waves = lax.psum(gradient_terms.reshape(wave_count, 2 * charges_width), "dom")
    back_waves = damping[:, None] * gradient_waves

    def indirect_step(running, first_wave):
        cosines, sines, wave_piece = phases_of(first_wave, wave_rows)
        back_piece = lax.dynamic_slice_in_dim(back_waves, first_wave, wave_rows, 0)
        return (
            running
            + (
                product(cosines, back_piece[:, :charges_width])
                + product(sines, back_piece[:, charges_width:])
            ),
            None,
        )

    indirect_sum, _ = lax.scan(
        indirect_step, jnp.zeros((atoms, charges_width), jnp.float32), first_waves
    )
    charge_grad = direct_sum + indirect_sum
    charge_rounded = charge_grad.astype(jnp.bfloat16)
    charge_sum = contract_first(hidden, charge_rounded)
    species_sum = contract_first(one_hot, charge_grad)
    upstream = contract_last(charge_rounded, charge_weight)
    before_grad = (upstream * silu_slope(before)).astype(jnp.bfloat16)
    mix_sum = contract_first(messages, before_grad)
    message_grad = contract_last(before_grad, mix_weight).astype(jnp.bfloat16)

    def radial_block(running, block_args):
        slot_rows, own_coords, live_count, rows_grad = block_args
        basis_rows, edge_weight = edge_terms(
            own_coords, coords_all[:, slot_rows], live_count, box_lengths, basis_count
        )
        edge_term = (
            edge_weight[..., None]
            * rows_grad.astype(jnp.float32)[:, None, :]
            * feature_table[slot_rows].astype(jnp.float32)
        ).astype(jnp.bfloat16)
        return (
            running
            + contract_first(basis_rows.reshape(-1, basis_count), edge_term.reshape(-1, width)),
            None,
        )

    radial_sum, _ = lax.scan(
        radial_block,
        jnp.zeros((basis_count, width), jnp.float32),
        (slot_blocks, own_blocks, count_blocks, message_grad.reshape(blocks, edge_rows, width)),
    )
    radial_total, mix_total, charge_total, species_total = lax.psum(
        (radial_sum, mix_sum, charge_sum, species_sum), "dom"
    )
    return (
        forces,
        normalized(radial_total),
        normalized(mix_total),
        normalized(charge_total),
        normalized(species_total),
    )


def solution(mesh):
    placed = (
        P(("cell", "dom"), None),
        P(None, ("cell", "dom")),
        P(("cell", "dom"), None),
        P(("cell", "dom")),
        P(None, ("cell", "dom")),
        P(("cell", "dom")),
        P(),
        P(None, ("cell", "dom")),
        P(),
        P(),
        P(),
        P(),
    )
    return jax.shard_map(
        on_device,
        mesh=mesh,
        in_specs=placed,
        out_specs=(
            P(None, ("cell", "dom")),
            P("cell", None),
            P("cell", None),
            P("cell", None),
            P("cell", None),
        ),
        check_vma=False,
    )
```

profile of v0, /device:TPU:8, one launch (start us, length us, event | category | flops | bytes accessed | tf_op | source)
XLA Modules:
  0.0 1416.6 jit_solution(16379144580854131616)
XLA Ops:
  9.6 3.8 collective-permute-start
  14.2 11.7 collective-permute-start.1
  26.6 1.9 gather_fusion.6
  28.5 1.9 collective-permute-start.2
  30.4 7.2 collective-permute-start.3
  41.5 101.1 %while.73 = (s32[]{:T(128)}, bf16[4,64,128]{2,1,0:T(8,128)(2,1)S(1)}, s32[4,64]{1,0:T(4,128)S(1)}, s32[4,64,64]{2,1,0:T(8,128)S(1)}, f32[3,768]{0,1:T(8,128)S(1)...) while((s32[]{:T(128)}, ...), condition=%wide.region_4.5_spmd.clone, body=%wide.region_1.0_spmd.sunk.clone.sunk | while | flops 19329056 | bytes 3677461 | solution.py:124
  41.6 10.8 gather_fusion.1
  53.4 12.1 gather_fusion
  65.5 1.2 fusion.167
  66.9 10.8 gather_fusion.1
  78.7 12.1 gather_fusion
  90.8 1.2 fusion.167
  92.2 10.8 gather_fusion.1
  103.9 12.1 gather_fusion
  116.1 1.2 fusion.167
  117.4 10.8 gather_fusion.1
  129.2 12.1 gather_fusion
  141.4 1.2 fusion.167
  143.4 22.4 %while.72 = (s32[]{:T(128)}, f32[4,256,128]{2,1,0:T(8,128)S(1)}, s32[4]{0:T(128)S(1)}, f32[3,1024]{1,0:T(4,128)S(1)}, f32[3,256]{1,0:T(4,128)S(1)}, /*index=5*/f...) while((s32[]{:T(128)}, f32[4,256,128]{2,1,0:T(8,128)S(1)}, s32[4]{0:T(128)S(1)}, ...), condition=%wide.region_6.7_spmd, body=%wide.region_5.6_spmd.sunk | while | flops 103055360 | bytes 1843347 | solution.py:167
  163.3 1.2 fusion.161
  166.9 263.0 %all-reduce.5.cloned.1.call-done = f32[1024,128]{1,0:T(8,128)} async-done(((f32[1024,128]{1,0:T(8,128)}), f32[1024,128]{1,0:T(8,128)}) %all-reduce.5.cloned.1.call-update) | async-done | bytes 524304 | tf_op jit(solution)/shard_map/psum | solution.py:168
  429.9 1.2 broadcast_multiply_fusion.1
  431.2 22.2 %while.74 = (s32[]{:T(128)}, f32[3,256]{1,0:T(4,128)S(1)}, s32[4]{0:T(128)S(1)}, f32[3,1024]{1,0:T(4,128)S(1)}, f32[3,256]{1,0:T(4,128)S(1)}, /*index=5*/f32[102...) while((s32[]{:T(128)}, f32[3,256]{1,0:T(4,128)S(1)}, ...), condition=%wide.region_9.10_spmd.clone, body=%wide.region_8.9_spmd.clone.sunk | while | flops 105580032 | bytes 2378949 | solution.py:175
  454.1 34.0 %while.75 = (s32[]{:T(128)}, f32[256,64]{0,1:T(8,128)S(1)}, f32[4,256,128]{2,1,0:T(8,128)S(1)}, s32[4]{0:T(128)S(1)}, f32[3,1024]{1,0:T(4,128)S(1)}, /*index=5*/...) while((s32[]{:T(128)}, f32[256,64]{0,1:T(8,128)S(1)}, ...), condition=%wide.region_11.12_spmd.clone, body=%wide.region_10.11_spmd.clone.sunk | while | flops 206405632 | bytes 4210905 | solution.py:191
  457.6 1.2 convolution_negate_fusion.2
  458.8 1.2 fusion.190
  466.1 1.2 convolution_negate_fusion.2
  467.3 1.2 fusion.190
  474.6 1.2 convolution_negate_fusion.2
  475.8 1.2 fusion.190
  483.2 1.2 convolution_negate_fusion.2
  484.4 1.2 fusion.190
  489.2 263.4 %all-reduce.7.cloned.1.call-done = f32[1024,128]{1,0:T(8,128)} async-done(((f32[1024,128]{1,0:T(8,128)}), f32[1024,128]{1,0:T(8,128)}) %all-reduce.7.cloned.1.call-update) | async-done | bytes 524304 | tf_op jit(solution)/shard_map/psum | solution.py:194
  752.6 1.2 broadcast_multiply_fusion
  753.9 21.6 %while.76 = (s32[]{:T(128)}, f32[256,64]{0,1:T(8,128)S(1)}, s32[4]{0:T(128)S(1)}, f32[3,1024]{1,0:T(4,128)S(1)}, f32[3,256]{1,0:T(4,128)S(1)}, /*index=5*/f32[10...) while((s32[]{:T(128)}, f32[256,64]{0,1:T(8,128)S(1)}, s32[4]{0:T(128)S(1)}, ...), condition=%wide.region_14.15_spmd.clone, body=%wide.region_13.14_spmd.clone.sunk | while | flops 103071744 | bytes 1319097 | solution.py:209
  777.1 99.2 %while.77 = (s32[]{:T(128)}, f32[16,128]{1,0:T(8,128)S(1)}, s32[4,64,64]{2,1,0:T(8,128)S(1)}, f32[3,768]{0,1:T(8,128)S(1)}, f32[4,3,64]{2,1,0:T(4,128)S(1)}, /*i...) while((s32[]{:T(128)}, f32[16,128]{1,0:T(8,128)S(1)}, ...), condition=%wide.region_17.18_spmd.clone.clone, body=%wide.region_15.17_spmd.sunk.clone.clone.sunk | while | flops 19349540 | bytes 3722535 | solution.py:237
  777.2 10.8 gather_fusion.3
  789.0 12.1 gather_fusion.2
  802.0 10.8 gather_fusion.3
  813.8 12.1 gather_fusion.2
  826.8 10.8 gather_fusion.3
  838.6 12.1 gather_fusion.2
  851.7 10.8 gather_fusion.3
  863.4 12.1 gather_fusion.2
  876.4 275.5 %all-reduce = (f32[16,128]{1,0:T(8,128)S(1)}, f32[128,64]{0,1:T(8,128)S(1)}, f32[6,64]{1,0:T(8,128)S(1)}) all-reduce(f32[16,128]{1,0:T(8,128)S(1)} %get-tuple-element.388, f32[128,64]{0,1:T(8,128)S(1)} %fusion.77, f32[6,64]{1,0:T(8,128)S(1)} %fusion.67), channel_id=1, replica_groups=mesh['dom'=64,'cell'=8] {'dom'}, use_global_device_ids=true, to_apply=%region_18.19 | all-reduce | flops 10624 | bytes 84992 | tf_op jit(solution)/shard_map/psum | solution.py:242
  1157.6 248.8 %all-reduce.9.cloned.1.call-done = f32[128,128]{1,0:T(8,128)} async-done(((f32[128,128]{1,0:T(8,128)}), f32[128,128]{1,0:T(8,128)}) %all-reduce.9.cloned.1.call-update) | async-done | bytes 65552 | tf_op jit(solution)/shard_map/psum | solution.py:242
  1406.4 1.5 multiply_reduce_fusion
  1408.6 1.5 broadcast_divide_fusion
  (261 shorter events, 85.6 us)
Async XLA Ops:
  7.2 135.4 %copy-start = (bf16[128,128]{1,0:T(8,128)(2,1)S(1)}, bf16[128,128]{1,0:T(8,128)(2,1)}, u32[]{:S(2)}) copy-start(bf16[128,128]{1,0:T(8,128)(2,1)} %param.34) | copy-start | bytes 98308
  7.2 34.3 %copy-start.6 = (f32[3]{0:T(128)S(1)}, f32[3]{0:T(128)}, u32[]{:S(2)}) copy-start(f32[3]{0:T(128)} %constant.233) | copy-start | bytes 40
  7.2 34.3 %copy-start.7 = (f32[3]{0:T(128)S(1)}, f32[3]{0:T(128)}, u32[]{:S(2)}) copy-start(f32[3]{0:T(128)} %constant.225.clone..sunk.5) | copy-start | bytes 40
  7.2 34.0 %copy-start.2 = (f32[3,256]{1,0:T(4,128)S(1)}, f32[3,256]{1,0:T(4,128)}, u32[]{:S(2)}) copy-start(f32[3,256]{1,0:T(4,128)} %param.26) | copy-start | bytes 9220
  7.2 34.2 %copy-start.1 = (bf16[256,128]{1,0:T(8,128)(2,1)S(1)}, bf16[256,128]{1,0:T(8,128)(2,1)}, u32[]{:S(2)}) copy-start(bf16[256,128]{1,0:T(8,128)(2,1)} %param.25) | copy-start | bytes 196612
  7.2 34.2 %copy-start.12 = (bf16[16,128]{1,0:T(8,128)(2,1)S(1)}, bf16[16,128]{1,0:T(8,128)(2,1)}, u32[]{:S(2)}) copy-start(bf16[16,128]{1,0:T(8,128)(2,1)} %param.33) | copy-start | bytes 12292
  7.2 422.7 %all-reduce.5.cloned.1.call-start = ((), (), s32[]{:S(2)}) async-start(), calls=%async_computation | async-start | bytes 1048576 | tf_op jit(solution)/shard_map/psum | solution.py:168
  9.6 31.4 %collective-permute-start = (f32[1,3,256]{1,2,0:T(8,128)S(1)}, f32[1,3,256]{1,2,0:T(8,128)S(1)}, u32[]{:S(2)}, u32[]{:S(2)}) collective-permute-start(f32[1,3,256]{1,2,0:T(8,128)S(1)} %bitcast.190), channel_id=1, source_target_pairs={{0,8},{8,16},{16,24},{24,32},{32,40},{40,48},{48,56},{56,64},{64,7... | collective-permute-start | bytes 9224 | tf_op jit(solution)/shard_map/ppermute | solution.py:21
  14.2 26.9 %collective-permute-start.1 = (f32[1,3,256]{1,2,0:T(8,128)S(1)}, f32[1,3,256]{1,2,0:T(8,128)S(1)}, u32[]{:S(2)}, u32[]{:S(2)}) collective-permute-start(f32[1,3,256]{1,2,0:T(8,128)S(1)} %bitcast.191), channel_id=1, source_target_pairs={{8,0},{16,8},{24,16},{32,24},{40,32},{48,40},{56,48},{64,56},{72,6... | collective-permute-start | bytes 9224 | tf_op jit(solution)/shard_map/ppermute | solution.py:22
  28.5 12.9 collective-permute-start.2
  30.4 11.0 collective-permute-start.3
  41.5 101.3 %copy-start.8 = (bf16[128,64]{0,1:T(8,128)(2,1)S(1)}, bf16[128,64]{0,1:T(8,128)(2,1)}, u32[]{:S(2)}) copy-start(bf16[128,64]{0,1:T(8,128)(2,1)} %param.35) | copy-start | bytes 49156
  41.5 101.5 %copy-start.9 = (s32[256]{0:T(256)S(1)}, s32[256]{0:T(256)}, u32[]{:S(2)}) copy-start(s32[256]{0:T(256)} %param.30) | copy-start | bytes 3076
  41.5 101.5 %copy-start.10 = (f32[6,64]{1,0:T(8,128)S(1)}, f32[6,64]{1,0:T(8,128)}, u32[]{:S(2)}) copy-start(f32[6,64]{1,0:T(8,128)} %param.36) | copy-start | bytes 4612
  165.9 0.8 copy-start.4
  166.7 586.0 %all-reduce.7.cloned.1.call-start = ((), (), s32[]{:S(2)}) async-start(), calls=%async_computation.1 | async-start | bytes 1048576 | tf_op jit(solution)/shard_map/psum | solution.py:194
  431.2 22.3 %copy-start.11 = (f32[3,256]{1,0:T(4,128)S(1)}, f32[3,256]{1,0:T(4,128)}, u32[]{:S(2)}) copy-start(f32[3,256]{1,0:T(4,128)} %param.32) | copy-start | bytes 9220
  453.4 0.6 copy-start.5
  488.1 0.8 copy-start.3
  488.9 917.5 %all-reduce.9.cloned.1.call-start = ((), (), s32[]{:S(2)}) async-start(), calls=%async_computation.2 | async-start | bytes 131072 | tf_op jit(solution)/shard_map/psum | solution.py:242
Sparse Core Ops, SparseCore 0:
  166.8 263.0 all-reduce.4
  489.0 263.5 all-reduce.6
  1155.2 251.1 all-reduce.8
where the time goes:
time: 1420 us
  waiting for transfers between devices  775 us (55%)
  blocking collectives  275 us (19%)
  local copies, waits for them, and re-layouts  209 us (15%)
  matrix products  68.3 us (5%)
  loops' own time  32.3 us (2%)
  starting transfers between devices  25.2 us (2%)
  between operations  17 us (1%)
    psum x1, blocking collectives, on_device(): lax.psum((radial_sum, mix_sum, charge_sum, species_sum), 'dom')  275 us
    psum x1, waiting for transfers between devices, on_device(): lax.psum(gradient_terms.reshape(wave_count, 2 * charges_width), 'dom')  263 us
    psum x1, waiting for transfers between devices, on_device(): structure = lax.psum(wave_terms, 'dom')  263 us
    psum x1, waiting for transfers between devices, on_device(): lax.psum((radial_sum, mix_sum, charge_sum, species_sum), 'dom')  249 us
    gather x4, local copies, waits for them, and re-layouts, message_block(): feature_table[slot_rows].astype(jnp.float32)  48.5 us
    gather x4, local copies, waits for them, and re-layouts, radial_block(): feature_table[slot_rows].astype(jnp.float32)  48.5 us
    gather x8, local copies, waits for them, and re-layouts, radial_block(): coords_all[:, slot_rows]  45.8 us
    gather x8, local copies, waits for them, and re-layouts, message_block(): coords_all[:, slot_rows]  45.8 us
  transfers between devices with their start and end apart: 7, of which 3 were waited for; matrix products, arithmetic and copies ran while one was open for 1% of the time, Pallas kernels for 0%

commit v1 on v0

v1 whole, which is shorter than its diff:
```python
import math

import jax
import jax.numpy as jnp
from jax import lax
from jax.experimental import pallas as pl
from jax.experimental.pallas import tpu as pltpu
from jax.sharding import PartitionSpec as P

f32 = jnp.float32
bf16 = jnp.bfloat16
MESH = pl.DeviceIdType.MESH

ATOM = 256
CHAN = 128
CHARGES = 64
WAVES = 1024
SLOTS = 64
BASIS = 16
SPECIES = 6
TABLE = 3 * ATOM
NX = 4
NZ = 16
DOMS = NX * NZ
TOTAL = ATOM * DOMS
XROWS = WAVES // NX
ZROWS = XROWS // NZ
PACK = 256
PROWS = PACK // NZ
SIDES = (1.25 * TOTAL / 64, 20.0, 20.0)
CUTOFF = 5.0
SPREAD = 2.0 * math.sqrt(math.log2(math.e))
CENTERS = [0.5 + 4.5 * b / 15 for b in range(BASIS)]
COS_QUARTER = [(-1.0) ** n * (math.pi / 2) ** (2 * n) / math.factorial(2 * n) for n in range(8)]
SIN_HALF = [(-1.0) ** n * math.pi ** (2 * n + 1) / math.factorial(2 * n + 1) for n in range(8)]
COS_HALF = [(-1.0) ** n * math.pi ** (2 * n) / math.factorial(2 * n) for n in range(9)]


def nn(left, right):
    return lax.dot_general(left, right, (((1,), (0,)), ((), ())), preferred_element_type=f32)


def nt(left, right):
    return lax.dot_general(left, right, (((1,), (1,)), ((), ())), preferred_element_type=f32)


def split(value):
    high = value.astype(bf16)
    return high, (value - high.astype(f32)).astype(bf16)


def poly(coeffs, square):
    total = jnp.full_like(square, coeffs[-1])
    for coeff in reversed(coeffs[:-1]):
        total = total * square + coeff
    return total


def iota(shape, dim):
    return lax.broadcasted_iota(jnp.int32, shape, dim)


def sum_all(value):
    return jnp.sum(jnp.sum(value, axis=1, keepdims=True), axis=0, keepdims=True)


def kernel(
    feat_ref, pos_ref, nbr_ref, cnt_ref, ghost_ref, spec_ref, wave_ref, fref_ref,
    rw_ref, mw_ref, cw_ref, sc_ref,
    forces_ref, rstep_ref, mstep_ref, cstep_ref, sstep_ref,
    wpad, wcol, ppad, pcol, tpad, cos_ref, sin_ref, idx_ref, bit_ref, word_ref,
    m_ref, ml_ref, g_ref, outf, outp, gf, gp,
    w1h, w1l, w2h, w2l, t1h, t1l, t2h, t2l, mix_ref, dir_ref,
    sx, rx, xown, sz, rz, res, sg, pk, rz3, xb3, res3,
    gsend, grecv, xsend, xrecv, zsend, zrecv, asend, arecv, bsend, brecv,
    z3send, z3recv, x3send, x3recv, a3send, a3recv,
):
    me = lax.axis_index("dom")
    xi = lax.div(me, NZ)
    zi = lax.rem(me, NZ)
    upper = lax.rem(me + 1, DOMS)
    lower = lax.rem(me + DOMS - 1, DOMS)

    def xpeer(off):
        return lax.rem(xi + off, NX) * NZ + zi

    def zat(off):
        return lax.rem(zi + off, NZ)

    def zpeer(off):
        return xi * NZ + zat(off)

    barrier = pltpu.get_barrier_semaphore()

    def greet(target):
        pl.semaphore_signal(barrier, inc=1, device_id={"dom": target}, device_id_type=MESH)

    def greet_z(off, carry):
        greet(zpeer(off))
        return carry

    lax.fori_loop(1, NZ, greet_z, 0)
    for off in range(1, NX):
        greet(xpeer(off))
    greet(upper)
    greet(lower)

    def remote(src, dst, send, recv, target):
        return pltpu.make_async_remote_copy(
            src_ref=src, dst_ref=dst, send_sem=send, recv_sem=recv,
            device_id={"dom": target}, device_id_type=MESH,
        )

    ft32 = feat_ref[...].astype(f32).T
    ftb = ft32.astype(bf16)
    tpad[...] = jnp.zeros_like(tpad)
    ppad[...] = jnp.zeros_like(ppad)
    ppad[0:3, :] = pos_ref[...]
    own8 = ppad[0:8, :]
    pcol[0:ATOM, :] = ppad[...].T
    p1 = own8.astype(bf16)
    p2 = (own8 - p1.astype(f32)).astype(bf16)
    p3 = (own8 - p1.astype(f32) - p2.astype(f32)).astype(bf16)
    rows_of = iota((ATOM, ATOM), 0)
    for r in range(2):
        perm = jnp.where(rows_of == ghost_ref[r : r + 1, :], 1.0, 0.0).astype(bf16)
        outf[r] = nn(ftb, perm).astype(bf16)
        outp[r] = nn(p1, perm) + nn(p2, perm) + nn(p3, perm)

    pl.semaphore_wait(barrier, NZ - 1 + NX - 1 + 2)

    ghost_copies = []
    for r, target in ((1, upper), (0, lower)):
        slot = 1 - r
        ghost_copies.append(
            remote(outp.at[r], gp.at[slot], gsend.at[2 * slot], grecv.at[2 * slot], target)
        )
        ghost_copies.append(
            remote(outf.at[r], gf.at[slot], gsend.at[2 * slot + 1], grecv.at[2 * slot + 1], target)
        )
    for copy in ghost_copies:
        copy.start()

    wave = wave_ref[...].astype(f32)
    wpad[...] = jnp.zeros_like(wpad)
    wpad[0:3, :] = wave
    steps = [2.0 * math.pi / side for side in SIDES]
    square = sum((wave[a : a + 1, :] * steps[a]) ** 2 for a in range(3))
    wpad[3:4, :] = jnp.exp(-0.5 * square) * (1.0 / TOTAL)
    wcol[...] = wpad[...].T

    pos = pos_ref[...]
    px, py, pz = (pos[a : a + 1, :] for a in range(3))
    tx, ty, tz = (pos[a : a + 1, :] * (1.0 / SIDES[a]) for a in range(3))

    def phase_block(step, carry):
        rows = pl.ds(pl.multiple_of(step * 32, 32), 32)
        cols = wcol[rows, :]
        turns = cols[:, 0:1] * tx + cols[:, 1:2] * ty + cols[:, 2:3] * tz
        turns = turns - jnp.floor(turns + 0.5)
        sq = turns * turns
        half_sin = turns * poly(SIN_HALF, sq)
        half_cos = poly(COS_HALF, sq)
        cos_ref[rows, :] = 1.0 - 2.0 * half_sin * half_sin
        sin_ref[rows, :] = 2.0 * half_sin * half_cos
        return carry

    lax.fori_loop(0, WAVES // 32, phase_block, 0)

    tpad[:, 0:SLOTS] = nbr_ref[0:128, :].astype(f32)
    left = tpad[...].T[0:SLOTS, :]
    tpad[:, 0:SLOTS] = nbr_ref[128:256, :].astype(f32)
    right = tpad[...].T[0:SLOTS, :]
    entries = jnp.concatenate([left, right], axis=1).astype(jnp.int32)
    live = iota((SLOTS, ATOM), 0) < cnt_ref[...]
    idx_ref[...] = jnp.where(live, lax.shift_right_logical(entries, 5), -1)
    bit_ref[...] = lax.shift_left(jnp.ones_like(entries), entries & 31)
    word_rows = iota((TABLE // 32, ATOM), 0)

    def word_step(n, words):
        hit = word_rows == idx_ref[pl.ds(n, 1), :]
        return words | jnp.where(hit, bit_ref[pl.ds(n, 1), :], 0)

    word_ref[...] = lax.fori_loop(
        0, SLOTS, word_step, jnp.zeros((TABLE // 32, ATOM), jnp.int32)
    )
    shifts = iota((32, ATOM), 0)

    def edge_block(step, carry):
        rows = pl.ds(pl.multiple_of(step * 32, 32), 32)
        cols = pcol[rows, :]
        dist2 = jnp.zeros((32, ATOM), f32)
        for a, own in enumerate((px, py, pz)):
            delta = cols[:, a : a + 1] - own
            delta = delta - SIDES[a] * jnp.floor(delta * (1.0 / SIDES[a]) + 0.5)
            dist2 = dist2 + delta * delta
        dist = jnp.sqrt(dist2)
        part = jnp.minimum(dist, CUTOFF) * (1.0 / CUTOFF)
        fade = poly(COS_QUARTER, part * part)
        mask = lax.shift_right_logical(
            jnp.broadcast_to(word_ref[pl.ds(step, 1), :], (32, ATOM)), shifts
        ) & 1
        weight = fade * fade * mask.astype(f32)
        scaled = dist * SPREAD
        for b in range(BASIS):
            away = scaled - SPREAD * CENTERS[b]
            basis = jnp.exp2(-(away * away)).astype(bf16)
            m_ref[b, rows, :], ml_ref[b, rows, :] = split(basis.astype(f32) * weight)
        return carry

    lax.fori_loop(0, ATOM // 32, edge_block, 0)

    for copy in ghost_copies:
        copy.wait_recv()
    for slot in range(2):
        ppad[0:8, :] = gp[slot]
        pcol[(1 + slot) * ATOM : (2 + slot) * ATOM, :] = ppad[...].T
    lax.fori_loop(ATOM // 32, TABLE // 32, edge_block, 0)

    tpad[...] = jnp.zeros_like(tpad)
    tpad[0:BASIS, :] = rw_ref[...].astype(f32)
    radial = tpad[...].T
    messages = jnp.zeros((CHAN, ATOM), f32)
    for b in range(BASIS):
        gathered = jnp.zeros((CHAN, ATOM), f32)
        for part in (m_ref, ml_ref):
            gathered = (
                gathered
                + nn(ftb, part[b, 0:ATOM, :])
                + nn(gf[0], part[b, ATOM : 2 * ATOM, :])
                + nn(gf[1], part[b, 2 * ATOM : TABLE, :])
            )
        g_ref[b] = gathered
        messages = messages + radial[:, b : b + 1] * gathered
    messages_b = messages.astype(bf16)
    mixT = mw_ref[...].astype(f32).T.astype(bf16)
    before = nn(mixT, messages_b)
    sigmoid = 1.0 / (1.0 + jnp.exp(-before))
    hidden_b = (ft32 + before * sigmoid).astype(bf16)
    slope = sigmoid * (1.0 + before * (1.0 - sigmoid))
    tpad[:, 0:CHARGES] = cw_ref[...].astype(f32)
    cwT = tpad[...].T[0:CHARGES, :].astype(bf16)
    tpad[...] = jnp.zeros_like(tpad)
    tpad[0:SPECIES, 0:CHARGES] = sc_ref[...]
    offsets = tpad[...].T[0:CHARGES, :]
    species = spec_ref[...]
    charges = nn(cwT, hidden_b)
    added = jnp.zeros((CHARGES, ATOM), f32)
    for s in range(SPECIES):
        added = jnp.where(species == s, offsets[:, s : s + 1], added)
    charges = charges + added
    qh, ql = split(charges)
    zero = jnp.zeros((CHARGES, ATOM), bf16)
    w1h[0:CHARGES, :] = qh
    w1h[CHARGES:CHAN, :] = zero
    w1l[0:CHARGES, :] = ql
    w1l[CHARGES:CHAN, :] = zero
    w2h[0:CHARGES, :] = zero
    w2h[CHARGES:CHAN, :] = qh
    w2l[0:CHARGES, :] = zero
    w2l[CHARGES:CHAN, :] = ql
    for source, target in ((w1h, t1h), (w1l, t1l), (w2h, t2h), (w2l, t2l)):
        target[...] = source[...].astype(f32).T.astype(bf16)

    def both(first, second, negate):
        fh, fl = split(first)
        sh, sl = split(second)
        one = nn(fh, t1h[...]) + nn(fh, t1l[...]) + nn(fl, t1h[...])
        two = nn(sh, t2h[...]) + nn(sh, t2l[...]) + nn(sl, t2h[...])
        return one - two if negate else one + two

    def chunk_rows(off):
        return pl.ds(pl.multiple_of(lax.rem(xi + off, NX) * XROWS, XROWS), XROWS)

    def z_rows(off):
        return pl.ds(pl.multiple_of(zat(off) * ZROWS, ZROWS), ZROWS)

    def res_rows(off):
        return pl.ds(pl.multiple_of(xi * XROWS + zat(off) * ZROWS, ZROWS), ZROWS)

    def x_copy(t, off):
        return remote(
            sx.at[t, off - 1], rx.at[t, off - 1], xsend.at[t, off - 1], xrecv.at[t, off - 1], xpeer(off)
        )

    def z_copy(t, off):
        return remote(
            sz.at[t, z_rows(off)], rz.at[t, off - 1], zsend.at[t, off - 1], zrecv.at[t, off - 1], zpeer(off)
        )

    def a_copy(t, off):
        mine = res_rows(0)
        return remote(
            res.at[t, mine], res.at[t, mine], asend.at[t, off - 1], arecv.at[t, off - 1], zpeer(off)
        )

    def a_arrival(t, off):
        theirs = res_rows(NZ - off)
        return remote(
            res.at[t, theirs], res.at[t, theirs], asend.at[t, off - 1], arecv.at[t, off - 1], zpeer(off)
        )

    def b_copy(t, off):
        rows = chunk_rows(0)
        return remote(
            res.at[t, rows], res.at[t, rows], bsend.at[t, off - 1], brecv.at[t, off - 1], xpeer(off)
        )

    def b_arrival(t, off):
        rows = chunk_rows(NX - off)
        return remote(
            res.at[t, rows], res.at[t, rows], bsend.at[t, off - 1], brecv.at[t, off - 1], xpeer(off)
        )

    def reduce_partials(t, partial):
        for off in (2, 1, 3):
            sx[t, off - 1] = partial(off).astype(bf16)
            x_copy(t, off).start()
        xown[...] = partial(0)
        for off in (1, 3, 2):
            x_copy(t, off).wait_recv()
            xown[...] = xown[...] + rx[t, off - 1].astype(f32)
        sz[t] = xown[...].astype(bf16)

        def z_start(off, carry):
            z_copy(t, off).start()
            return carry

        lax.fori_loop(1, NZ, z_start, 0)

        def z_take(off, total):
            z_copy(t, off).wait_recv()
            return total + rz[t, off - 1].astype(f32)

        total = lax.fori_loop(1, NZ, z_take, xown[z_rows(0), :])
        res[t, res_rows(0), :] = total.astype(bf16)

        def a_start(off, carry):
            a_copy(t, off).start()
            return carry

        def a_take(off, carry):
            a_arrival(t, off).wait_recv()
            return carry

        lax.fori_loop(1, NZ, a_start, 0)
        lax.fori_loop(1, NZ, a_take, 0)
        for off in (2, 1, 3):
            b_copy(t, off).start()

    def structure(off):
        rows = chunk_rows(off)
        return both(cos_ref[rows, :], sin_ref[rows, :], False)

    reduce_partials(0, structure)

    force = jnp.zeros((8, ATOM), f32)
    for off in (0, 1, 3, 2):
        if off:
            b_arrival(0, off).wait_recv()
        rows = chunk_rows(NX - off)
        damp = wcol[rows, 3:4]
        coeff = res[0, rows, :]
        along_cos = nn(coeff, w1h[...]) + nn(coeff, w1l[...])
        along_sin = nn(coeff, w2h[...]) + nn(coeff, w2l[...])
        mixture = damp * (sin_ref[rows, :] * along_cos - cos_ref[rows, :] * along_sin)
        mh, ml = split(mixture)
        index = wpad[0:8, rows].astype(bf16)
        force = force + nn(index, mh) + nn(index, ml)
    pulls = []
    for a in range(3):
        row = force[a : a + 1, :] * steps[a]
        forces_ref[a : a + 1, :] = row
        pulls.append(2.0 * (row - fref_ref[a : a + 1, :]) * steps[a])

    dir_ref[...] = jnp.zeros_like(dir_ref)

    def gradient(off):
        rows = chunk_rows(off)
        cols = wcol[rows, :]
        slopes = cols[:, 0:1] * pulls[0] + cols[:, 1:2] * pulls[1] + cols[:, 2:3] * pulls[2]
        along_sin = slopes * sin_ref[rows, :]
        along_cos = slopes * cos_ref[rows, :]
        return along_sin, along_cos, cols[:, 3:4]

    def wave_term(off):
        along_sin, along_cos, damp = gradient(off)
        return both(along_sin, along_cos, True)

    reduce_partials(1, wave_term)

    for off in (0, 1, 3, 2):
        rows = chunk_rows(NX - off)
        along_sin, along_cos, damp = gradient(NX - off)
        coeff = res[0, rows, :].astype(f32).T.astype(bf16)
        sh, sl = split(damp * along_sin)
        ch, cl = split(damp * along_cos)
        direct = nn(coeff, sh) + nn(coeff, sl)
        minus = nn(coeff, ch) + nn(coeff, cl)
        dir_ref[...] = dir_ref[...] + (direct[0:CHARGES] - minus[CHARGES:CHAN])
        if off:
            b_arrival(1, off).wait_recv()
        back = res[1, rows, :].astype(f32).T.astype(bf16)
        ch, cl = split(damp * cos_ref[rows, :])
        sh, sl = split(damp * sin_ref[rows, :])
        first = nn(back, ch) + nn(back, cl)
        second = nn(back, sh) + nn(back, sl)
        dir_ref[...] = dir_ref[...] + (first[0:CHARGES] + second[CHARGES:CHAN])
    charge_grad = dir_ref[...]
    rounded = charge_grad.astype(bf16)
    pk[128:192, :] = nt(rounded, hidden_b)
    kinds = jnp.where(iota((8, ATOM), 0) == species, 1.0, 0.0).astype(bf16)
    gh, gl = split(charge_grad)
    pk[208:PACK, :] = jnp.zeros((PACK - 208, CHAN), f32)
    pk[208:216, 0:CHARGES] = nt(kinds, gh) + nt(kinds, gl)
    upstream = nn(cw_ref[...], rounded)
    before_grad = (upstream * slope).astype(bf16)
    pk[0:128, :] = nt(messages_b, before_grad)
    message_grad = nn(mw_ref[...], before_grad).astype(bf16).astype(f32)
    lane = iota((CHAN, CHAN), 1)
    radial_sum = jnp.zeros((CHAN, CHAN), f32)
    for b in range(BASIS):
        column = jnp.sum(message_grad * g_ref[b], axis=1, keepdims=True)
        radial_sum = jnp.where(lane == b, column, radial_sum)
    pk[192:208, :] = radial_sum.T[0:BASIS, :]

    def p_rows(off):
        return pl.ds(pl.multiple_of(zat(off) * PROWS, PROWS), PROWS)

    def z3_copy(off):
        return remote(sg.at[p_rows(off)], rz3.at[off - 1], z3send.at[off - 1], z3recv.at[off - 1], zpeer(off))

    def x3_copy(off):
        return remote(xb3.at[xi], xb3.at[xi], x3send.at[off - 1], x3recv.at[off - 1], xpeer(off))

    def x3_arrival(off):
        theirs = lax.rem(xi + NX - off, NX)
        return remote(xb3.at[theirs], xb3.at[theirs], x3send.at[off - 1], x3recv.at[off - 1], xpeer(off))

    def a3_copy(off):
        mine = p_rows(0)
        return remote(res3.at[mine], res3.at[mine], a3send.at[off - 1], a3recv.at[off - 1], zpeer(off))

    def a3_arrival(off):
        theirs = p_rows(NZ - off)
        return remote(res3.at[theirs], res3.at[theirs], a3send.at[off - 1], a3recv.at[off - 1], zpeer(off))

    sg[...] = pk[...].astype(bf16)

    def z3_start(off, carry):
        z3_copy(off).start()
        return carry

    def z3_take(off, total):
        z3_copy(off).wait_recv()
        return total + rz3[off - 1].astype(f32)

    lax.fori_loop(1, NZ, z3_start, 0)
    xb3[xi] = lax.fori_loop(1, NZ, z3_take, pk[p_rows(0), :])
    for off in (2, 1, 3):
        x3_copy(off).start()
    for off in (1, 3, 2):
        x3_arrival(off).wait_recv()
    res3[p_rows(0), :] = (xb3[0] + xb3[1] + xb3[2] + xb3[3]).astype(bf16)

    def a3_start(off, carry):
        a3_copy(off).start()
        return carry

    def a3_take(off, carry):
        a3_arrival(off).wait_recv()
        return carry

    lax.fori_loop(1, NZ, a3_start, 0)
    lax.fori_loop(1, NZ, a3_take, 0)

    def scaled(value, count):
        return value / jnp.sqrt(sum_all(value * value) * (1.0 / count) + 1e-06)

    mstep_ref[...] = scaled(res3[0:128, :].astype(f32), CHAN * CHAN)
    tpad[...] = jnp.zeros_like(tpad)
    tpad[0:CHARGES, :] = scaled(res3[128:192, :].astype(f32), CHAN * CHARGES)
    cstep_ref[...] = tpad[...].T[:, 0:CHARGES]
    rstep_ref[...] = scaled(res3[192:208, :].astype(f32), BASIS * CHAN)
    tail = scaled(res3[208:224, :].astype(f32), SPECIES * CHARGES)
    sstep_ref[...] = tail[0:SPECIES, 0:CHARGES]

    for copy in ghost_copies:
        copy.wait_send()
    for t in range(2):
        for off in range(1, NX):
            x_copy(t, off).wait_send()
            b_copy(t, off).wait_send()
    for off in range(1, NX):
        x3_copy(off).wait_send()

    def drain(off, carry):
        for t in range(2):
            z_copy(t, off).wait_send()
            a_copy(t, off).wait_send()
        z3_copy(off).wait_send()
        a3_copy(off).wait_send()
        return carry

    lax.fori_loop(1, NZ, drain, 0)


def on_device(
    features, positions, neighbours, neighbour_count, ghost_sends, species,
    wave_index, force_ref, radial_weight, mix_weight, charge_weight, species_charge,
):
    dma = pltpu.SemaphoreType.DMA
    vmem = pltpu.VMEM
    wide = [vmem((CHAN, ATOM), bf16)] * 4 + [vmem((ATOM, CHAN), bf16)] * 4
    scratch = [
        vmem((128, WAVES), f32),
        vmem((WAVES, 128), f32),
        vmem((128, ATOM), f32),
        vmem((TABLE, 128), f32),
        vmem((128, 128), f32),
        vmem((WAVES, ATOM), f32),
        vmem((WAVES, ATOM), f32),
        vmem((SLOTS, ATOM), jnp.int32),
        vmem((SLOTS, ATOM), jnp.int32),
        vmem((TABLE // 32, ATOM), jnp.int32),
        vmem((BASIS, TABLE, ATOM), bf16),
        vmem((BASIS, TABLE, ATOM), bf16),
        vmem((BASIS, CHAN, ATOM), f32),
        vmem((2, CHAN, ATOM), bf16),
        vmem((2, 8, ATOM), f32),
        vmem((2, CHAN, ATOM), bf16),
        vmem((2, 8, ATOM), f32),
        *wide,
        vmem((8, ATOM), f32),
        vmem((CHARGES, ATOM), f32),
        vmem((2, NX - 1, XROWS, CHAN), bf16),
        vmem((2, NX - 1, XROWS, CHAN), bf16),
        vmem((XROWS, CHAN), f32),
        vmem((2, XROWS, CHAN), bf16),
        vmem((2, NZ - 1, ZROWS, CHAN), bf16),
        vmem((2, WAVES, CHAN), bf16),
        vmem((PACK, CHAN), bf16),
        vmem((PACK, CHAN), f32),
        vmem((NZ - 1, PROWS, CHAN), bf16),
        vmem((NX, PROWS, CHAN), f32),
        vmem((PACK, CHAN), bf16),
        dma((4,)),
        dma((4,)),
        dma((2, NX - 1)),
        dma((2, NX - 1)),
        dma((2, NZ - 1)),
        dma((2, NZ - 1)),
        dma((2, NZ - 1)),
        dma((2, NZ - 1)),
        dma((2, NX - 1)),
        dma((2, NX - 1)),
        dma((NZ - 1,)),
        dma((NZ - 1,)),
        dma((NX - 1,)),
        dma((NX - 1,)),
        dma((NZ - 1,)),
        dma((NZ - 1,)),
    ]
    spec = pl.BlockSpec(memory_space=pltpu.VMEM)
    return pl.pallas_call(
        kernel,
        out_shape=(
            jax.ShapeDtypeStruct((3, ATOM), f32),
            jax.ShapeDtypeStruct((BASIS, CHAN), f32),
            jax.ShapeDtypeStruct((CHAN, CHAN), f32),
            jax.ShapeDtypeStruct((CHAN, CHARGES), f32),
            jax.ShapeDtypeStruct((SPECIES, CHARGES), f32),
        ),
        in_specs=[spec] * 12,
        out_specs=(spec,) * 5,
        scratch_shapes=scratch,
        compiler_params=pltpu.CompilerParams(
            collective_id=0, has_side_effects=True, vmem_limit_bytes=48 * 1024 * 1024
        ),
        name="step",
    )(
        features,
        positions,
        neighbours,
        neighbour_count.reshape(1, ATOM),
        ghost_sends,
        species.reshape(1, ATOM),
        wave_index,
        force_ref,
        radial_weight,
        mix_weight,
        charge_weight,
        species_charge,
    )


def solution(mesh):
    placed = (
        P(("cell", "dom"), None),
        P(None, ("cell", "dom")),
        P(("cell", "dom"), None),
        P(("cell", "dom")),
        P(None, ("cell", "dom")),
        P(("cell", "dom")),
        P(),
        P(None, ("cell", "dom")),
        P(),
        P(),
        P(),
        P(),
    )
    return jax.shard_map(
        on_device,
        mesh=mesh,
        in_specs=placed,
        out_specs=(
            P(None, ("cell", "dom")),
            P("cell", None),
            P("cell", None),
            P("cell", None),
            P("cell", None),
        ),
        check_vma=False,
    )
```

time: 1420 us -> 114 us (0.08)
  waiting for transfers between devices: 775 us -> 0 us
  blocking collectives: 275 us -> 0 us
  local copies, waits for them, and re-layouts: 209 us -> 4.99 us
  Pallas kernels: 0 us -> 108 us
  matrix products: 68.3 us -> 0 us
  loops' own time: 32.3 us -> 0 us
  starting transfers between devices: 25.2 us -> 0 us
  between operations: 17 us -> 0.81 us
    psum x3 -> x0, waiting for transfers between devices: 775 us -> none  [the longest x1 263 us: on_device(): lax.psum(gradient_terms.reshape(wave_count, 2 * charges_width), 'dom')]
    psum x1 -> x0, blocking collectives: 275 us -> none  [on_device(): lax.psum((radial_sum, mix_sum, charge_sum, species_sum), 'dom')]
    gather x27 -> x0, local copies, waits for them, and re-layouts: 192 us -> none  [the longest x4 48.5 us: message_block(): feature_table[slot_rows].astype(jnp.float32)]
    pallas_call x0 -> x1, Pallas kernels: none -> 108 us  [on_device(): pl.pallas_call(kernel, out_shape=(jax.ShapeDtypeStruct((3, ATOM), f32), j...]
    dot_general x80 -> x0, matrix products: 68.3 us -> none  [the longest x43 33.8 us: contract_first(): lax.dot_general(left, right, (((0,), (0,)), ((), ())), precision=highest,...]
    another operation x6 -> x0, loops' own time: 32.3 us -> none  [the longest x1 8.02 us: on_device(): lax.scan(gradient_step, jnp.zeros((atoms, charges_width), jnp.float32), f...]
    ppermute x4 -> x0, starting transfers between devices: 24.7 us -> none  [the longest x2 18.9 us: extended(): after = lax.ppermute(initial, axis, down)]
  transfers between devices with their start and end apart: 7 -> 0, of which waited for: 3 -> 0; matrix products, arithmetic and copies ran while one was open for 1% -> 0% of each run, Pallas kernels for 0% -> 0%
where the time goes in v1:
time: 114 us
  Pallas kernels  108 us (95%)
  local copies, waits for them, and re-layouts  4.99 us (4%)
    pallas_call x1, Pallas kernels, on_device(): pl.pallas_call(kernel, out_shape=(jax.ShapeDtypeStruct((3, ATOM), f32), j...  108 us
    unnamed x26, local copies, waits for them, and re-layouts  4.29 us

profile of v1, /device:TPU:8, one launch (start us, length us, event | category | flops | bytes accessed | tf_op | source)
XLA Modules:
  0.0 113.8 jit_solution(8775042647904630477)
XLA Ops:
  0.6 0.8 copy.18.cw_ref
  1.5 0.0 copy-start
  1.5 0.0 copy-start.1
  1.5 0.0 copy-start.2
  1.5 0.0 copy-start.3
  1.5 0.0 copy-start.4
  1.5 0.0 copy-start.5
  1.5 0.0 copy-start.6
  1.5 0.0 copy-start.7
  1.6 0.0 copy-start.8
  1.6 0.0 copy-start.9
  1.6 1.0 copy.17.nbr_ref
  2.6 0.0 copy-done
  2.6 0.0 copy-done.1
  2.6 0.0 copy-done.2
  2.6 0.0 copy-done.3
  2.6 0.0 copy-done.4
  2.6 0.0 copy-done.5
  2.6 0.0 copy-done.6
  2.6 0.0 copy-done.7
  2.7 0.0 copy-done.8
  2.7 0.0 copy-done.9
  2.7 108.0 %step.1 = (f32[3,256]{1,0:T(4,128)S(1)}, f32[16,128]{1,0:T(8,128)S(1)}, f32[128,128]{1,0:T(8,128)S(1)}, f32[128,64]{1,0:T(8,128)S(1)}, f32[6,64]{1,0:T(8,128)S(1)}) custom-call(bf16[256,128]{1,0:T(8,128)(2,1)S(1)} %copy-done, f32[3,256]{1,0:T(4,128)S(1)} %copy-done.3, s32[256,64]{1,0:T(8,128)S(1)} %copy.17.nbr_ref, s32[1,256]{1,0:T(1,128)S(1)} %bitcast.2, ...), custom_call_target="tpu_custom_call" | custom-call | tf_op jit(solution)/shard_map/step/pallas_call | solution.py:565
  110.7 0.7 copy.19
  111.4 0.6 copy.24
  112.0 0.6 copy.25
  112.6 0.6 copy.26
  113.2 0.6 copy.27
Async XLA Ops:
  1.5 1.1 copy-start
  1.5 1.1 copy-start.1
  1.5 1.1 copy-start.2
  1.5 1.1 copy-start.3
  1.5 1.1 copy-start.4
  1.5 1.1 copy-start.5
  1.5 1.1 copy-start.6
  1.5 1.1 copy-start.7
  1.6 1.1 copy-start.8
  1.6 1.1 copy-start.9

commit v2 on v1

v2 whole, which is shorter than its diff:
```python
import math

import jax
import jax.numpy as jnp
from jax import lax
from jax.experimental import pallas as pl
from jax.experimental.pallas import tpu as pltpu
from jax.sharding import PartitionSpec as P

f32 = jnp.float32
bf16 = jnp.bfloat16
MESH = pl.DeviceIdType.MESH

ATOM = 256
CHAN = 128
CHARGES = 64
WAVES = 1024
SLOTS = 64
BASIS = 16
SPECIES = 6
TABLE = 3 * ATOM
NX = 4
NZ = 16
DOMS = NX * NZ
TOTAL = ATOM * DOMS
XROWS = WAVES // NX
ZROWS = XROWS // NZ
PACK = 256
PROWS = PACK // NZ
SIDES = (1.25 * TOTAL / 64, 20.0, 20.0)
CUTOFF = 5.0
SPREAD = 2.0 * math.sqrt(math.log2(math.e))
CENTERS = [0.5 + 4.5 * b / 15 for b in range(BASIS)]
COS_QUARTER = [(-1.0) ** n * (math.pi / 2) ** (2 * n) / math.factorial(2 * n) for n in range(8)]
SIN_HALF = [(-1.0) ** n * math.pi ** (2 * n + 1) / math.factorial(2 * n + 1) for n in range(8)]
COS_HALF = [(-1.0) ** n * math.pi ** (2 * n) / math.factorial(2 * n) for n in range(9)]


def nn(left, right):
    return lax.dot_general(left, right, (((1,), (0,)), ((), ())), preferred_element_type=f32)


def nt(left, right):
    return lax.dot_general(left, right, (((1,), (1,)), ((), ())), preferred_element_type=f32)


def split(value):
    high = value.astype(bf16)
    return high, (value - high.astype(f32)).astype(bf16)


def poly(coeffs, square):
    total = jnp.full_like(square, coeffs[-1])
    for coeff in reversed(coeffs[:-1]):
        total = total * square + coeff
    return total


def iota(shape, dim):
    return lax.broadcasted_iota(jnp.int32, shape, dim)


def sum_all(value):
    return jnp.sum(jnp.sum(value, axis=1, keepdims=True), axis=0, keepdims=True)


def kernel(
    feat_ref, pos_ref, nbr_ref, cnt_ref, ghost_ref, spec_ref, wave_ref, fref_ref,
    rw_ref, mw_ref, cwt_ref, sc_ref,
    forces_ref, total_ref,
    wpad, wcol, kb, ppad, pcol, tpad, cos_ref, sin_ref, ch_ref, cl_ref, sh_ref, sl_ref,
    ssh_ref, ssl_ref, sch_ref, scl_ref, idx_ref, bit_ref, word_ref,
    m_ref, ml_ref, g_ref, outf, outp, gf, gp,
    xpos, qall, tq, fsend, frecv, cg_ref, cgs, cgr,
    wave32, sz, rz, res, sg, pk, rz3, xb3, res3,
    gsend, grecv, psend, precv, qsend, qrecv, fsem, frsem, csend, crecv,
    zsend, zrecv, asend, arecv, z3send, z3recv, x3send, x3recv, a3send, a3recv,
):
    me = lax.axis_index("dom")
    xi = lax.div(me, NZ)
    zi = lax.rem(me, NZ)
    upper = lax.rem(me + 1, DOMS)
    lower = lax.rem(me + DOMS - 1, DOMS)

    def xpeer(off):
        return lax.rem(xi + off, NX) * NZ + zi

    def zat(off):
        return lax.rem(zi + off, NZ)

    def far_first(step):
        return NZ // 2 + (1 - 2 * lax.rem(step, 2)) * lax.div(step + 1, 2)

    def zpeer(off):
        return xi * NZ + zat(off)

    barrier = pltpu.get_barrier_semaphore()

    def greet(target):
        pl.semaphore_signal(barrier, inc=1, device_id={"dom": target}, device_id_type=MESH)

    def greet_z(step, carry):
        greet(zpeer(far_first(step)))
        return carry

    lax.fori_loop(0, NZ - 1, greet_z, 0)
    for off in range(1, NX):
        greet(xpeer(off))
    greet(upper)
    greet(lower)

    def remote(src, dst, send, recv, target):
        return pltpu.make_async_remote_copy(
            src_ref=src, dst_ref=dst, send_sem=send, recv_sem=recv,
            device_id={"dom": target}, device_id_type=MESH,
        )

    ft32 = feat_ref[...].astype(f32).T
    ftb = ft32.astype(bf16)
    tpad[...] = jnp.zeros_like(tpad)
    ppad[...] = jnp.zeros_like(ppad)
    ppad[0:3, :] = pos_ref[...]
    own8 = ppad[0:8, :]
    pcol[0:ATOM, :] = ppad[...].T
    p1 = own8.astype(bf16)
    p2 = (own8 - p1.astype(f32)).astype(bf16)
    p3 = (own8 - p1.astype(f32) - p2.astype(f32)).astype(bf16)
    rows_of = iota((ATOM, ATOM), 0)
    for r in range(2):
        perm = jnp.where(rows_of == ghost_ref[r : r + 1, :], 1.0, 0.0).astype(bf16)
        outf[r] = nn(ftb, perm).astype(bf16)
        outp[r] = nn(p1, perm) + nn(p2, perm) + nn(p3, perm)
    xpos[0] = own8
    xpos[0, 3:6, :] = fref_ref[...]

    wave = wave_ref[...].astype(f32)
    wpad[...] = jnp.zeros_like(wpad)
    wpad[0:3, :] = wave
    steps = [2.0 * math.pi / side for side in SIDES]
    square = sum((wave[a : a + 1, :] * steps[a]) ** 2 for a in range(3))
    wpad[3:4, :] = jnp.exp(-0.5 * square) * (1.0 / TOTAL)
    mine = pl.ds(pl.multiple_of(xi * XROWS, XROWS), XROWS)
    wcol[...] = wpad[:, mine].T
    damp_col = jnp.broadcast_to(wcol[:, 3:4], (XROWS, 128))
    kb[3] = damp_col
    for a in range(3):
        spread = jnp.broadcast_to(wcol[:, a : a + 1], (XROWS, 128))
        kb[a] = spread
        kb[4 + a] = spread * damp_col

    def twice(value):
        return jnp.concatenate([value, value], axis=1)

    def phases(block):
        own = xpos[block]
        tx, ty, tz = (own[a : a + 1, :] * (1.0 / SIDES[a]) for a in range(3))

        def phase_block(step, carry):
            rows = pl.ds(pl.multiple_of(step * 32, 32), 32)
            turns = (
                twice(kb[0, rows, :]) * tx + twice(kb[1, rows, :]) * ty + twice(kb[2, rows, :]) * tz
            )
            turns = turns - jnp.floor(turns + 0.5)
            sq = turns * turns
            half_sin = turns * poly(SIN_HALF, sq)
            half_cos = poly(COS_HALF, sq)
            cosine = 1.0 - 2.0 * half_sin * half_sin
            sine = 2.0 * half_sin * half_cos
            cos_ref[block, rows, :] = cosine
            sin_ref[block, rows, :] = sine
            ch_ref[block, rows, :], cl_ref[block, rows, :] = split(cosine)
            sh_ref[block, rows, :], sl_ref[block, rows, :] = split(sine)
            return carry

        lax.fori_loop(0, XROWS // 32, phase_block, 0)

    phases(0)

    entries = nbr_ref[...]
    live = iota((SLOTS, ATOM), 0) < cnt_ref[...]
    idx_ref[...] = jnp.where(live, lax.shift_right_logical(entries, 5), -1)
    bit_ref[...] = lax.shift_left(jnp.ones_like(entries), entries & 31)
    word_rows = iota((TABLE // 32, ATOM), 0)

    def word_step(n, words):
        hit = word_rows == idx_ref[pl.ds(n, 1), :]
        return words | jnp.where(hit, bit_ref[pl.ds(n, 1), :], 0)

    word_ref[...] = lax.fori_loop(
        0, SLOTS, word_step, jnp.zeros((TABLE // 32, ATOM), jnp.int32)
    )

    pl.semaphore_wait(barrier, NZ - 1 + NX - 1 + 2)

    ghost_copies = []
    for r, target in ((1, upper), (0, lower)):
        slot = 1 - r
        ghost_copies.append(
            remote(outp.at[r], gp.at[slot], gsend.at[2 * slot], grecv.at[2 * slot], target)
        )
        ghost_copies.append(
            remote(outf.at[r], gf.at[slot], gsend.at[2 * slot + 1], grecv.at[2 * slot + 1], target)
        )

    def x_message(src, dst_ref, send, recv, off):
        return remote(src, dst_ref.at[off], send.at[off - 1], recv.at[off - 1], xpeer(off))

    for copy in ghost_copies:
        copy.start()
    pos_copies = {off: x_message(xpos.at[0], xpos, psend, precv, off) for off in (2, 1, 3)}
    for copy in pos_copies.values():
        copy.start()

    px, py, pz = (pos_ref[a : a + 1, :] for a in range(3))
    shifts = iota((32, ATOM), 0)

    def edge_block(step, carry):
        rows = pl.ds(pl.multiple_of(step * 32, 32), 32)
        cols = pcol[rows, :]
        dist2 = jnp.zeros((32, ATOM), f32)
        for a, own in enumerate((px, py, pz)):
            delta = cols[:, a : a + 1] - own
            delta = delta - SIDES[a] * jnp.floor(delta * (1.0 / SIDES[a]) + 0.5)
            dist2 = dist2 + delta * delta
        dist = jnp.sqrt(dist2)
        part = jnp.minimum(dist, CUTOFF) * (1.0 / CUTOFF)
        fade = poly(COS_QUARTER, part * part)
        mask = lax.shift_right_logical(
            jnp.broadcast_to(word_ref[pl.ds(step, 1), :], (32, ATOM)), shifts
        ) & 1
        weight = fade * fade * mask.astype(f32)
        scaled = dist * SPREAD
        for b in range(BASIS):
            away = scaled - SPREAD * CENTERS[b]
            basis = jnp.exp2(-(away * away)).astype(bf16)
            m_ref[b, rows, :], ml_ref[b, rows, :] = split(basis.astype(f32) * weight)
        return carry

    lax.fori_loop(0, ATOM // 32, edge_block, 0)
    for b in range(BASIS):
        g_ref[b] = nn(ftb, m_ref[b, 0:ATOM, :]) + nn(ftb, ml_ref[b, 0:ATOM, :])

    for copy in ghost_copies:
        copy.wait_recv()
    for slot in range(2):
        ppad[0:8, :] = gp[slot]
        pcol[(1 + slot) * ATOM : (2 + slot) * ATOM, :] = ppad[...].T
    lax.fori_loop(ATOM // 32, TABLE // 32, edge_block, 0)

    tpad[0:BASIS, :] = rw_ref[...].astype(f32)
    radial = tpad[...].T
    messages = jnp.zeros((CHAN, ATOM), f32)
    for b in range(BASIS):
        gathered = g_ref[b]
        for part in (m_ref, ml_ref):
            gathered = (
                gathered
                + nn(gf[0], part[b, ATOM : 2 * ATOM, :])
                + nn(gf[1], part[b, 2 * ATOM : TABLE, :])
            )
        g_ref[b] = gathered
        messages = messages + radial[:, b : b + 1] * gathered
    messages_b = messages.astype(bf16)
    mixT = mw_ref[...].astype(f32).T.astype(bf16)
    before = nn(mixT, messages_b)
    sigmoid = 1.0 / (1.0 + jnp.exp(-before))
    hidden_b = (ft32 + before * sigmoid).astype(bf16)
    slope = sigmoid * (1.0 + before * (1.0 - sigmoid))
    cwT = cwt_ref[...]
    tpad[0:CHARGES, :] = cwT.astype(f32)
    cw = tpad[...].T[:, 0:CHARGES].astype(bf16)
    tpad[...] = jnp.zeros_like(tpad)
    tpad[0:SPECIES, 0:CHARGES] = sc_ref[...]
    offsets = tpad[...].T[0:CHARGES, :]
    species = spec_ref[...]
    charges = nn(cwT, hidden_b)
    added = jnp.zeros((CHARGES, ATOM), f32)
    for s in range(SPECIES):
        added = jnp.where(species == s, offsets[:, s : s + 1], added)
    qall[0, 0:CHARGES, :], qall[0, CHARGES:CHAN, :] = split(charges + added)
    charge_copies = {off: x_message(qall.at[0], qall, qsend, qrecv, off) for off in (2, 1, 3)}
    for copy in charge_copies.values():
        copy.start()

    for off in (1, 3, 2):
        pos_copies[off].wait_recv()
        phases(off)

    lane = iota((XROWS, CHAN), 1)

    def fold(one, two):
        one = one + pltpu.roll(one, CHARGES, 1)
        two = two + pltpu.roll(two, CHARGES, 1)
        return jnp.where(lane < CHARGES, one, two)

    def z_rows(off):
        return pl.ds(pl.multiple_of(zat(off) * ZROWS, ZROWS), ZROWS)

    def z_copy(t, off):
        return remote(
            sz.at[t, z_rows(off)], rz.at[t, off - 1], zsend.at[t, off - 1], zrecv.at[t, off - 1], zpeer(off)
        )

    def a_copy(t, off):
        rows = z_rows(0)
        return remote(
            res.at[t, rows], res.at[t, rows], asend.at[t, off - 1], arecv.at[t, off - 1], zpeer(off)
        )

    def a_arrival(t, off):
        rows = z_rows(NZ - off)
        return remote(
            res.at[t, rows], res.at[t, rows], asend.at[t, off - 1], arecv.at[t, off - 1], zpeer(off)
        )

    def reduce_start(t, partial):
        wave32[...] = partial
        sz[t] = partial.astype(bf16)

        def z_start(step, carry):
            z_copy(t, far_first(step)).start()
            return carry

        lax.fori_loop(0, NZ - 1, z_start, 0)

    def reduce_finish(t):
        def z_take(step, total):
            off = far_first(NZ - 2 - step)
            z_copy(t, off).wait_recv()
            return total + rz[t, off - 1].astype(f32)

        total = lax.fori_loop(0, NZ - 1, z_take, wave32[z_rows(0), :])
        res[t, z_rows(0), :] = total.astype(bf16)

        def a_start(step, carry):
            a_copy(t, far_first(step)).start()
            return carry

        lax.fori_loop(0, NZ - 1, a_start, 0)

    def gather_finish(t):
        def a_take(step, carry):
            a_arrival(t, far_first(NZ - 2 - step)).wait_recv()
            return carry

        lax.fori_loop(0, NZ - 1, a_take, 0)

    one = jnp.zeros((XROWS, CHAN), f32)
    two = jnp.zeros((XROWS, CHAN), f32)
    for s in (0, 1, 3, 2):
        if s:
            charge_copies[s].wait_recv()
        tq[s] = qall[s].astype(f32).T.astype(bf16)
        one = one + nn(ch_ref[s], tq[s]) + nn(cl_ref[s], tq[s])
        two = two + nn(sh_ref[s], tq[s]) + nn(sl_ref[s], tq[s])
    reduce_start(0, fold(one, two))
    reduce_finish(0)
    gather_finish(0)

    coeff = res[0].astype(f32)
    swapped = pltpu.roll(coeff, CHARGES, 1)
    cos_pair = jnp.where(lane < CHARGES, coeff, swapped).astype(bf16)
    sin_pair = jnp.where(lane < CHARGES, swapped, coeff).astype(bf16)

    def at_x(s):
        return lax.rem(xi + NX - s, NX)

    for s in range(NX):
        mixture = sin_ref[s] * nn(cos_pair, qall[s]) - cos_ref[s] * nn(sin_pair, qall[s])
        for a in range(3):
            row = jnp.sum(twice(kb[4 + a]) * mixture, axis=0, keepdims=True)
            fsend[pl.ds(a * NX + at_x(s), 1), :] = row
    force_copies = {
        off: remote(fsend, frecv.at[off - 1], fsem.at[off - 1], frsem.at[off - 1], xpeer(off))
        for off in (2, 1, 3)
    }
    for copy in force_copies.values():
        copy.start()

    def paired(value):
        high, low = split(value)
        first = jnp.concatenate([high[0:CHARGES], low[0:CHARGES]], axis=0)
        second = jnp.concatenate([high[CHARGES:CHAN], low[CHARGES:CHAN]], axis=0)
        return first, second

    coeff_cos, coeff_sin = paired((kb[3] * coeff).T)

    for off in (1, 3, 2):
        force_copies[off].wait_recv()
    pulls = []
    for s in range(NX):
        rows = []
        for a in range(3):
            at = pl.ds(a * NX + at_x(s), 1)
            row = fsend[at, :] + frecv[0, at, :] + frecv[1, at, :] + frecv[2, at, :]
            row = row * steps[a]
            if s == 0:
                forces_ref[a : a + 1, :] = row
            rows.append(2.0 * (row - xpos[s, 3 + a : 4 + a, :]) * steps[a])
        pulls.append(rows)

    one = jnp.zeros((XROWS, CHAN), f32)
    two = jnp.zeros((XROWS, CHAN), f32)
    for s in range(NX):
        slopes = (
            twice(kb[0]) * pulls[s][0] + twice(kb[1]) * pulls[s][1] + twice(kb[2]) * pulls[s][2]
        )
        ssh_ref[s], ssl_ref[s] = split(slopes * sin_ref[s])
        sch_ref[s], scl_ref[s] = split(slopes * cos_ref[s])
        one = one + nn(ssh_ref[s], tq[s]) + nn(ssl_ref[s], tq[s])
        two = two + nn(sch_ref[s], tq[s]) + nn(scl_ref[s], tq[s])
    reduce_start(1, fold(one, -two))

    for s in range(NX):
        direct = (
            nn(coeff_cos, ssh_ref[s]) + nn(coeff_cos, ssl_ref[s])
            - nn(coeff_sin, sch_ref[s]) - nn(coeff_sin, scl_ref[s])
        )
        cg_ref[s] = direct[0:CHARGES] + direct[CHARGES:CHAN]
    reduce_finish(1)
    gather_finish(1)
    back_cos, back_sin = paired((kb[3] * res[1].astype(f32)).T)

    def charge_part(s):
        back = (
            nn(back_cos, ch_ref[s]) + nn(back_cos, cl_ref[s])
            + nn(back_sin, sh_ref[s]) + nn(back_sin, sl_ref[s])
        )
        return cg_ref[s] + (back[0:CHARGES] + back[CHARGES:CHAN])

    owner_copies = {}
    for s in (2, 1, 3):
        cgs[s - 1] = charge_part(s).astype(bf16)
        owner_copies[s] = remote(
            cgs.at[s - 1], cgr.at[s - 1], csend.at[s - 1], crecv.at[s - 1], xpeer(NX - s)
        )
        owner_copies[s].start()
    charge_grad = charge_part(0)
    for s in (1, 3, 2):
        owner_copies[s].wait_recv()
        charge_grad = charge_grad + cgr[s - 1].astype(f32)

    rounded = charge_grad.astype(bf16)
    pk[128:192, :] = nt(rounded, hidden_b)
    kinds = jnp.where(iota((8, ATOM), 0) == species, 1.0, 0.0).astype(bf16)
    gh, gl = split(charge_grad)
    pk[208:PACK, :] = jnp.zeros((PACK - 208, CHAN), f32)
    pk[208:216, 0:CHARGES] = nt(kinds, gh) + nt(kinds, gl)
    upstream = nn(cw, rounded)
    before_grad = (upstream * slope).astype(bf16)
    pk[0:128, :] = nt(messages_b, before_grad)
    message_grad = nn(mw_ref[...], before_grad).astype(bf16).astype(f32)
    lanes = iota((CHAN, CHAN), 1)
    radial_sum = jnp.zeros((CHAN, CHAN), f32)
    for b in range(BASIS):
        column = jnp.sum(message_grad * g_ref[b], axis=1, keepdims=True)
        radial_sum = jnp.where(lanes == b, column, radial_sum)
    pk[192:208, :] = radial_sum.T[0:BASIS, :]

    def p_rows(off):
        return pl.ds(pl.multiple_of(zat(off) * PROWS, PROWS), PROWS)

    def z3_copy(off):
        return remote(sg.at[p_rows(off)], rz3.at[off - 1], z3send.at[off - 1], z3recv.at[off - 1], zpeer(off))

    def x3_copy(off):
        return remote(xb3.at[xi], xb3.at[xi], x3send.at[off - 1], x3recv.at[off - 1], xpeer(off))

    def x3_arrival(off):
        theirs = lax.rem(xi + NX - off, NX)
        return remote(xb3.at[theirs], xb3.at[theirs], x3send.at[off - 1], x3recv.at[off - 1], xpeer(off))

    def a3_copy(off):
        mine = p_rows(0)
        return remote(res3.at[mine], res3.at[mine], a3send.at[off - 1], a3recv.at[off - 1], zpeer(off))

    def a3_arrival(off):
        theirs = p_rows(NZ - off)
        return remote(res3.at[theirs], res3.at[theirs], a3send.at[off - 1], a3recv.at[off - 1], zpeer(off))

    sg[...] = pk[...].astype(bf16)

    def z3_start(step, carry):
        z3_copy(far_first(step)).start()
        return carry

    def z3_take(step, total):
        off = far_first(NZ - 2 - step)
        z3_copy(off).wait_recv()
        return total + rz3[off - 1].astype(f32)

    lax.fori_loop(0, NZ - 1, z3_start, 0)
    xb3[xi] = lax.fori_loop(0, NZ - 1, z3_take, pk[p_rows(0), :])
    for off in (2, 1, 3):
        x3_copy(off).start()
    for off in (1, 3, 2):
        x3_arrival(off).wait_recv()
    res3[p_rows(0), :] = (xb3[0] + xb3[1] + xb3[2] + xb3[3]).astype(bf16)

    def a3_start(step, carry):
        a3_copy(far_first(step)).start()
        return carry

    def a3_take(step, carry):
        a3_arrival(far_first(NZ - 2 - step)).wait_recv()
        return carry

    lax.fori_loop(0, NZ - 1, a3_start, 0)
    lax.fori_loop(0, NZ - 1, a3_take, 0)

    total_ref[...] = res3[...]

    for copy in ghost_copies:
        copy.wait_send()
    for copies in (pos_copies, charge_copies, force_copies, owner_copies):
        for copy in copies.values():
            copy.wait_send()
    for off in range(1, NX):
        x3_copy(off).wait_send()

    def drain(off, carry):
        for t in range(2):
            z_copy(t, off).wait_send()
            a_copy(t, off).wait_send()
        z3_copy(off).wait_send()
        a3_copy(off).wait_send()
        return carry

    lax.fori_loop(1, NZ, drain, 0)


def finish(
    raw_ref, total_ref, forces_ref, rstep_ref, mstep_ref, cstep_ref, sstep_ref
):
    def scaled(rows, count):
        value = total_ref[rows, :].astype(f32)
        return value / jnp.sqrt(sum_all(value * value) * (1.0 / count) + 1e-06)

    forces_ref[...] = raw_ref[...]
    mstep_ref[...] = scaled(slice(0, 128), CHAN * CHAN)
    cstep_ref[...] = scaled(slice(128, 192), CHAN * CHARGES)
    rstep_ref[...] = scaled(slice(192, 208), BASIS * CHAN)
    sstep_ref[...] = scaled(slice(208, 224), SPECIES * CHARGES)[0:SPECIES, 0:CHARGES]


def on_device(
    features, positions, neighbours, neighbour_count, ghost_sends, species,
    wave_index, force_ref, radial_weight, mix_weight, charge_weight, species_charge,
):
    dma = pltpu.SemaphoreType.DMA
    vmem = pltpu.VMEM
    scratch = [
        vmem((128, WAVES), f32),
        vmem((XROWS, 128), f32),
        vmem((7, XROWS, 128), f32),
        vmem((128, ATOM), f32),
        vmem((TABLE, 128), f32),
        vmem((128, 128), f32),
        *[vmem((NX, XROWS, ATOM), f32)] * 2,
        *[vmem((NX, XROWS, ATOM), bf16)] * 8,
        vmem((SLOTS, ATOM), jnp.int32),
        vmem((SLOTS, ATOM), jnp.int32),
        vmem((TABLE // 32, ATOM), jnp.int32),
        vmem((BASIS, TABLE, ATOM), bf16),
        vmem((BASIS, TABLE, ATOM), bf16),
        vmem((BASIS, CHAN, ATOM), f32),
        vmem((2, CHAN, ATOM), bf16),
        vmem((2, 8, ATOM), f32),
        vmem((2, CHAN, ATOM), bf16),
        vmem((2, 8, ATOM), f32),
        vmem((NX, 8, ATOM), f32),
        vmem((NX, CHAN, ATOM), bf16),
        vmem((NX, ATOM, CHAN), bf16),
        vmem((16, ATOM), f32),
        vmem((NX - 1, 16, ATOM), f32),
        vmem((NX, CHARGES, ATOM), f32),
        vmem((NX - 1, CHARGES, ATOM), bf16),
        vmem((NX - 1, CHARGES, ATOM), bf16),
        vmem((XROWS, CHAN), f32),
        vmem((2, XROWS, CHAN), bf16),
        vmem((2, NZ - 1, ZROWS, CHAN), bf16),
        vmem((2, XROWS, CHAN), bf16),
        vmem((PACK, CHAN), bf16),
        vmem((PACK, CHAN), f32),
        vmem((NZ - 1, PROWS, CHAN), bf16),
        vmem((NX, PROWS, CHAN), f32),
        vmem((PACK, CHAN), bf16),
        dma((4,)),
        dma((4,)),
        *[dma((NX - 1,))] * 8,
        *[dma((2, NZ - 1))] * 4,
        dma((NZ - 1,)),
        dma((NZ - 1,)),
        dma((NX - 1,)),
        dma((NX - 1,)),
        dma((NZ - 1,)),
        dma((NZ - 1,)),
    ]
    spec = pl.BlockSpec(memory_space=pltpu.VMEM)
    raw, total = pl.pallas_call(
        kernel,
        out_shape=(
            jax.ShapeDtypeStruct((3, ATOM), f32),
            jax.ShapeDtypeStruct((PACK, CHAN), bf16),
        ),
        in_specs=[spec] * 12,
        out_specs=(spec,) * 2,
        scratch_shapes=scratch,
        compiler_params=pltpu.CompilerParams(
            collective_id=0, has_side_effects=True, vmem_limit_bytes=48 * 1024 * 1024
        ),
        name="step",
    )(
        features,
        positions,
        neighbours.T,
        neighbour_count.reshape(1, ATOM),
        ghost_sends,
        species.reshape(1, ATOM),
        wave_index,
        force_ref,
        radial_weight,
        mix_weight,
        charge_weight.T,
        species_charge,
    )
    forces, rstep, mstep, cstep, sstep = pl.pallas_call(
        finish,
        out_shape=(
            jax.ShapeDtypeStruct((3, ATOM), f32),
            jax.ShapeDtypeStruct((BASIS, CHAN), f32),
            jax.ShapeDtypeStruct((CHAN, CHAN), f32),
            jax.ShapeDtypeStruct((CHARGES, CHAN), f32),
            jax.ShapeDtypeStruct((SPECIES, CHARGES), f32),
        ),
        in_specs=[spec] * 2,
        out_specs=(spec,) * 5,
        name="finish",
    )(raw, total)
    return forces, rstep, mstep, cstep.T, sstep


def solution(mesh):
    placed = (
        P(("cell", "dom"), None),
        P(None, ("cell", "dom")),
        P(("cell", "dom"), None),
        P(("cell", "dom")),
        P(None, ("cell", "dom")),
        P(("cell", "dom")),
        P(),
        P(None, ("cell", "dom")),
        P(),
        P(),
        P(),
        P(),
    )
    return jax.shard_map(
        on_device,
        mesh=mesh,
        in_specs=placed,
        out_specs=(
            P(None, ("cell", "dom")),
            P("cell", None),
            P("cell", None),
            P("cell", None),
            P("cell", None),
        ),
        check_vma=False,
    )
```

time: 114 us -> 101 us (0.89)
  Pallas kernels: 108 us -> 91.1 us
  local copies, waits for them, and re-layouts: 4.99 us -> 8.49 us
    pallas_call x1, Pallas kernels: 108 us -> 89.5 us  [on_device(): pl.pallas_call(kernel, out_shape=(jax.ShapeDtypeStruct((3, ATOM), f32), j...]
    unnamed x26 -> x28, local copies, waits for them, and re-layouts: 4.29 us -> 8.49 us
    pallas_call x0 -> x1, Pallas kernels: none -> 1.62 us  [on_device(): pl.pallas_call(finish, out_shape=(jax.ShapeDtypeStruct((3, ATOM), f32), j...]
where the time goes in v2:
time: 101 us; the launch traced here: 100 us
  Pallas kernels  91.1 us (90%)
  local copies, waits for them, and re-layouts  8.49 us (8%)
    pallas_call x1, Pallas kernels, on_device(): pl.pallas_call(kernel, out_shape=(jax.ShapeDtypeStruct((3, ATOM), f32), j...  89.5 us
    unnamed x28, local copies, waits for them, and re-layouts  8.49 us

profile of v2, /device:TPU:8, one launch (start us, length us, event | category | flops | bytes accessed | tf_op | source)
XLA Modules:
  0.0 100.3 jit_solution(17510101085139541802)
XLA Ops:
  0.6 0.0 copy-start.6
  0.6 0.0 copy-start.11
  0.7 0.0 copy-start.12
  0.7 0.7 copy-done.6
  1.3 0.0 copy-done.11
  1.3 0.0 copy-done.12
  1.3 0.0 copy-start
  1.4 0.8 copy-done
  2.2 0.0 copy-start.1
  2.2 0.8 copy-done.1
  3.0 0.0 copy-start.3
  3.0 0.8 copy-done.3
  3.8 0.0 copy-start.4
  3.8 0.7 copy-done.4
  4.5 0.0 copy-start.5
  4.5 0.7 copy-done.5
  5.2 0.0 copy-start.7
  5.2 0.7 copy-done.7
  5.9 0.0 copy-start.8
  5.9 0.7 copy-done.8
  6.6 0.0 copy-start.9
  6.6 0.7 copy-done.9
  7.3 0.0 copy-start.13
  7.3 0.7 copy-done.13
  8.0 89.5 %step.1 = (f32[3,256]{1,0:T(4,128)S(1)}, bf16[256,128]{1,0:T(8,128)(2,1)S(1)}) custom-call(bf16[256,128]{1,0:T(8,128)(2,1)S(1)} %copy-done, f32[3,256]{1,0:T(4,128)S(1)} %copy-done.6, s32[64,256]{1,0:T(8,128)S(1)} %bitcast.5, s32[1,256]{1,0:T(1,128)S(1)} %bitcast.7, s32[2,256]{1,0:T(2,128)S(1)} %copy-done.11, s32[1,256]{1,0:T(1,128)S(1)} %bitcast.8, ...), custom_call_target="tpu_custom_call" | custom-call | tf_op jit(solution)/shard_map/step/pallas_call | solution.py:600
  97.4 0.0 copy-start.2
  97.4 0.6 copy-done.2
  98.0 0.0 copy-start.10
  98.0 0.6 copy-done.10
  98.6 1.6 %finish.1 = (f32[3,256]{1,0:T(4,128)}, f32[16,128]{1,0:T(8,128)}, f32[128,128]{1,0:T(8,128)}, f32[64,128]{1,0:T(8,128)}, f32[6,64]{1,0:T(8,128)}) custom-call(f32[3,256]{1,0:T(4,128)} %copy-done.10, bf16[256,128]{1,0:T(8,128)(2,1)} %copy-done.2), custom_call_target="tpu_custom_call" | custom-call | tf_op jit(solution)/shard_map/finish/pallas_call | solution.py:627
Async XLA Ops:
  0.6 0.7 copy-start.6
  0.6 0.7 copy-start.11
  0.7 0.7 copy-start.12
  1.3 0.8 copy-start
  2.2 0.8 copy-start.1
  3.0 0.8 copy-start.3
  3.8 0.7 copy-start.4
  4.5 0.7 copy-start.5
  5.2 0.7 copy-start.7
  5.9 0.7 copy-start.8
  6.6 0.7 copy-start.9
  7.3 0.7 copy-start.13
  97.4 0.6 copy-start.2
  98.0 0.6 copy-start.10

commit v3 on v2

--- a/solution.py
+++ b/solution.py
@@ -65,17 +65,29 @@
 
 
 def kernel(
+    feat_in, pos_in, nbr_in, cnt_in, ghost_in, spec_in, wave_in, fref_in,
+    rw_in, mw_in, cwt_in, sc_in,
+    forces_ref, total_ref,
     feat_ref, pos_ref, nbr_ref, cnt_ref, ghost_ref, spec_ref, wave_ref, fref_ref,
-    rw_ref, mw_ref, cwt_ref, sc_ref,
-    forces_ref, total_ref,
+    rw_ref, mw_ref, cwt_ref, sc_ref, in_sem,
     wpad, wcol, kb, ppad, pcol, tpad, cos_ref, sin_ref, ch_ref, cl_ref, sh_ref, sl_ref,
     ssh_ref, ssl_ref, sch_ref, scl_ref, idx_ref, bit_ref, word_ref,
-    m_ref, ml_ref, g_ref, outf, outp, gf, gp,
+    weight_ref, scaled_ref, m_ref, ml_ref, g_ref, outf, outp, gf, gp,
     xpos, qall, tq, fsend, frecv, cg_ref, cgs, cgr,
     wave32, sz, rz, res, sg, pk, rz3, xb3, res3,
-    gsend, grecv, psend, precv, qsend, qrecv, fsem, frsem, csend, crecv,
+    rounds, gsend, grecv, psend, precv, qsend, qrecv, fsem, frsem, csend, crecv,
     zsend, zrecv, asend, arecv, z3send, z3recv, x3send, x3recv, a3send, a3recv,
 ):
+    fetches = [
+        pltpu.make_async_copy(src, dst, in_sem.at[i])
+        for i, (src, dst) in enumerate((
+            (feat_in, feat_ref), (pos_in, pos_ref), (ghost_in, ghost_ref), (fref_in, fref_ref),
+            (wave_in, wave_ref), (nbr_in, nbr_ref), (cnt_in, cnt_ref), (rw_in, rw_ref),
+            (mw_in, mw_ref), (cwt_in, cwt_ref), (sc_in, sc_ref), (spec_in, spec_ref),
+        ))
+    ]
+    for copy in fetches:
+        copy.start()
     me = lax.axis_index("dom")
     xi = lax.div(me, NZ)
     zi = lax.rem(me, NZ)
@@ -99,21 +111,30 @@
     def greet(target):
         pl.semaphore_signal(barrier, inc=1, device_id={"dom": target}, device_id_type=MESH)
 
-    def greet_z(step, carry):
-        greet(zpeer(far_first(step)))
-        return carry
-
-    lax.fori_loop(0, NZ - 1, greet_z, 0)
     for off in range(1, NX):
         greet(xpeer(off))
     greet(upper)
     greet(lower)
+    greet(zpeer(1))
+    greet(zpeer(NZ - 1))
+
+    def reach_tell(level):
+        for off in (2**level, NZ - 2**level):
+            pl.semaphore_signal(
+                rounds.at[level], inc=1, device_id={"dom": zpeer(off)}, device_id_type=MESH
+            )
+
+    def reach_learn(level):
+        pl.semaphore_wait(rounds.at[level], 2)
 
     def remote(src, dst, send, recv, target):
         return pltpu.make_async_remote_copy(
             src_ref=src, dst_ref=dst, send_sem=send, recv_sem=recv,
             device_id={"dom": target}, device_id_type=MESH,
         )
+
+    for copy in fetches:
+        copy.wait()
 
     ft32 = feat_ref[...].astype(f32).T
     ftb = ft32.astype(bf16)
@@ -133,6 +154,29 @@
     xpos[0] = own8
     xpos[0, 3:6, :] = fref_ref[...]
 
+    pl.semaphore_wait(barrier, NX - 1 + 4)
+
+    ghost_copies = []
+    for r, target in ((1, upper), (0, lower)):
+        slot = 1 - r
+        ghost_copies.append(
+            remote(outp.at[r], gp.at[slot], gsend.at[2 * slot], grecv.at[2 * slot], target)
+        )
+        ghost_copies.append(
+            remote(outf.at[r], gf.at[slot], gsend.at[2 * slot + 1], grecv.at[2 * slot + 1], target)
+        )
+
+    def x_message(src, dst_ref, send, recv, off):
+        return remote(src, dst_ref.at[off], send.at[off - 1], recv.at[off - 1], xpeer(off))
+
+    for copy in ghost_copies:
+        copy.start()
+    pos_copies = {off: x_message(xpos.at[0], xpos, psend, precv, off) for off in (2, 1, 3)}
+    for copy in pos_copies.values():
+        copy.start()
+
+    reach_tell(0)
+
     wave = wave_ref[...].astype(f32)
     wpad[...] = jnp.zeros_like(wpad)
     wpad[0:3, :] = wave
@@ -190,26 +234,8 @@
         0, SLOTS, word_step, jnp.zeros((TABLE // 32, ATOM), jnp.int32)
     )
 
-    pl.semaphore_wait(barrier, NZ - 1 + NX - 1 + 2)
-
-    ghost_copies = []
-    for r, target in ((1, upper), (0, lower)):
-        slot = 1 - r
-        ghost_copies.append(
-            remote(outp.at[r], gp.at[slot], gsend.at[2 * slot], grecv.at[2 * slot], target)
-        )
-        ghost_copies.append(
-            remote(outf.at[r], gf.at[slot], gsend.at[2 * slot + 1], grecv.at[2 * slot + 1], target)
-        )
-
-    def x_message(src, dst_ref, send, recv, off):
-        return remote(src, dst_ref.at[off], send.at[off - 1], recv.at[off - 1], xpeer(off))
-
-    for copy in ghost_copies:
-        copy.start()
-    pos_copies = {off: x_message(xpos.at[0], xpos, psend, precv, off) for off in (2, 1, 3)}
-    for copy in pos_copies.values():
-        copy.start()
+    reach_learn(0)
+    reach_tell(1)
 
     px, py, pz = (pos_ref[a : a + 1, :] for a in range(3))
     shifts = iota((32, ATOM), 0)
@@ -228,17 +254,26 @@
         mask = lax.shift_right_logical(
             jnp.broadcast_to(word_ref[pl.ds(step, 1), :], (32, ATOM)), shifts
         ) & 1
-        weight = fade * fade * mask.astype(f32)
-        scaled = dist * SPREAD
+        weight_ref[rows, :] = fade * fade * mask.astype(f32)
+        scaled_ref[rows, :] = dist * SPREAD
+        return carry
+
+    def edge_sums(block, feats):
         for b in range(BASIS):
-            away = scaled - SPREAD * CENTERS[b]
-            basis = jnp.exp2(-(away * away)).astype(bf16)
-            m_ref[b, rows, :], ml_ref[b, rows, :] = split(basis.astype(f32) * weight)
-        return carry
+            for start in range(0, ATOM, 32):
+                at = pl.ds(block * ATOM + start, 32)
+                away = scaled_ref[at, :] - SPREAD * CENTERS[b]
+                basis = jnp.exp2(-(away * away)).astype(bf16).astype(f32)
+                high, low = split(basis * weight_ref[at, :])
+                m_ref[b, start : start + 32, :] = high
+                ml_ref[b, start : start + 32, :] = low
+            fresh = nn(feats, m_ref[b]) + nn(feats, ml_ref[b])
+            g_ref[b] = fresh if block == 0 else g_ref[b] + fresh
 
     lax.fori_loop(0, ATOM // 32, edge_block, 0)
-    for b in range(BASIS):
-        g_ref[b] = nn(ftb, m_ref[b, 0:ATOM, :]) + nn(ftb, ml_ref[b, 0:ATOM, :])
+    edge_sums(0, ftb)
+    reach_learn(1)
+    reach_tell(2)
 
     for copy in ghost_copies:
         copy.wait_recv()
@@ -246,20 +281,14 @@
         ppad[0:8, :] = gp[slot]
         pcol[(1 + slot) * ATOM : (2 + slot) * ATOM, :] = ppad[...].T
     lax.fori_loop(ATOM // 32, TABLE // 32, edge_block, 0)
+    edge_sums(1, gf[0])
+    edge_sums(2, gf[1])
 
     tpad[0:BASIS, :] = rw_ref[...].astype(f32)
     radial = tpad[...].T
     messages = jnp.zeros((CHAN, ATOM), f32)
     for b in range(BASIS):
-        gathered = g_ref[b]
-        for part in (m_ref, ml_ref):
-            gathered = (
-                gathered
-                + nn(gf[0], part[b, ATOM : 2 * ATOM, :])
-                + nn(gf[1], part[b, 2 * ATOM : TABLE, :])
-            )
-        g_ref[b] = gathered
-        messages = messages + radial[:, b : b + 1] * gathered
+        messages = messages + radial[:, b : b + 1] * g_ref[b]
     messages_b = messages.astype(bf16)
     mixT = mw_ref[...].astype(f32).T.astype(bf16)
     before = nn(mixT, messages_b)
@@ -353,6 +382,7 @@
         tq[s] = qall[s].astype(f32).T.astype(bf16)
         one = one + nn(ch_ref[s], tq[s]) + nn(cl_ref[s], tq[s])
         two = two + nn(sh_ref[s], tq[s]) + nn(sl_ref[s], tq[s])
+    reach_learn(2)
     reduce_start(0, fold(one, two))
     reduce_finish(0)
     gather_finish(0)
@@ -550,6 +580,19 @@
     dma = pltpu.SemaphoreType.DMA
     vmem = pltpu.VMEM
     scratch = [
+        vmem((ATOM, CHAN), bf16),
+        vmem((3, ATOM), f32),
+        vmem((SLOTS, ATOM), jnp.int32),
+        vmem((1, ATOM), jnp.int32),
+        vmem((2, ATOM), jnp.int32),
+        vmem((1, ATOM), jnp.int32),
+        vmem((3, WAVES), jnp.int32),
+        vmem((3, ATOM), f32),
+        vmem((BASIS, CHAN), bf16),
+        vmem((CHAN, CHAN), bf16),
+        vmem((CHARGES, CHAN), bf16),
+        vmem((SPECIES, CHARGES), f32),
+        dma((12,)),
         vmem((128, WAVES), f32),
         vmem((XROWS, 128), f32),
         vmem((7, XROWS, 128), f32),
@@ -561,8 +604,10 @@
         vmem((SLOTS, ATOM), jnp.int32),
         vmem((SLOTS, ATOM), jnp.int32),
         vmem((TABLE // 32, ATOM), jnp.int32),
-        vmem((BASIS, TABLE, ATOM), bf16),
-        vmem((BASIS, TABLE, ATOM), bf16),
+        vmem((TABLE, ATOM), f32),
+        vmem((TABLE, ATOM), f32),
+        vmem((BASIS, ATOM, ATOM), bf16),
+        vmem((BASIS, ATOM, ATOM), bf16),
         vmem((BASIS, CHAN, ATOM), f32),
         vmem((2, CHAN, ATOM), bf16),
         vmem((2, 8, ATOM), f32),
@@ -585,6 +630,7 @@
         vmem((NZ - 1, PROWS, CHAN), bf16),
         vmem((NX, PROWS, CHAN), f32),
         vmem((PACK, CHAN), bf16),
+        pltpu.SemaphoreType.REGULAR((3,)),
         dma((4,)),
         dma((4,)),
         *[dma((NX - 1,))] * 8,
@@ -603,11 +649,11 @@
             jax.ShapeDtypeStruct((3, ATOM), f32),
             jax.ShapeDtypeStruct((PACK, CHAN), bf16),
         ),
-        in_specs=[spec] * 12,
+        in_specs=[pl.BlockSpec(memory_space=pltpu.HBM)] * 12,
         out_specs=(spec,) * 2,
         scratch_shapes=scratch,
         compiler_params=pltpu.CompilerParams(
-            collective_id=0, has_side_effects=True, vmem_limit_bytes=48 * 1024 * 1024
+            collective_id=0, has_side_effects=True, vmem_limit_bytes=67043328
         ),
         name="step",
     )(
@@ -635,6 +681,7 @@
         ),
         in_specs=[spec] * 2,
         out_specs=(spec,) * 5,
+        compiler_params=pltpu.CompilerParams(vmem_limit_bytes=67043328),
         name="finish",
     )(raw, total)
     return forces, rstep, mstep, cstep.T, sstep

time: 101 us -> 89.1 us (0.88)
  local copies, waits for them, and re-layouts: 8.49 us -> 0 us
  Pallas kernels: 91.1 us -> 88.2 us
    unnamed x28 -> x0, local copies, waits for them, and re-layouts: 8.49 us -> none
    pallas_call x1, Pallas kernels: 89.5 us -> 86.6 us  [on_device(): pl.pallas_call(kernel, out_shape=(jax.ShapeDtypeStruct((3, ATOM), f32), j...]
where the time goes in v3:
time: 89.1 us; the launch traced here: 88.9 us
  Pallas kernels  88.2 us (99%)
    pallas_call x1, Pallas kernels, on_device(): pl.pallas_call(kernel, out_shape=(jax.ShapeDtypeStruct((3, ATOM), f32), j...  86.6 us

profile of v3, /device:TPU:8, one launch (start us, length us, event | category | flops | bytes accessed | tf_op | source)
XLA Modules:
  0.0 88.9 jit_solution(2232521667416883407)
XLA Ops:
  0.6 86.6 %step.1 = (f32[3,256]{1,0:T(4,128)}, bf16[256,128]{1,0:T(8,128)(2,1)}) custom-call(bf16[256,128]{1,0:T(8,128)(2,1)} %feat_in.1, f32[3,256]{1,0:T(4,128)} %pos_in.1, s32[64,256]{1,0:T(8,128)} %bitcast.5, s32[1,256]{1,0:T(1,128)} %bitcast.7, s32[2,256]{1,0:T(2,128)} %ghost_in.1, s32[1,256]{1,0:T(1,128)} %bitcast.8, s32[3,1024]{1,0:T(4,128)} %wave_in.1, ...), custom_call_target="tpu_custom_call" | custom-call | tf_op jit(solution)/shard_map/step/pallas_call | solution.py:646
  87.3 1.6 %finish.1 = (f32[3,256]{1,0:T(4,128)}, f32[16,128]{1,0:T(8,128)}, f32[128,128]{1,0:T(8,128)}, f32[64,128]{1,0:T(8,128)}, f32[6,64]{1,0:T(8,128)}) custom-call(f32[3,256]{1,0:T(4,128)} %get-tuple-element.12.raw_ref, bf16[256,128]{1,0:T(8,128)(2,1)} %get-tuple-element.13.total_ref), custom_call_target="tpu_custom_call" | custom-call | tf_op jit(solution)/shard_map/finish/pallas_call | solution.py:673

commit v4 on v3

--- a/solution.py
+++ b/solution.py
@@ -30,6 +30,9 @@
 SIDES = (1.25 * TOTAL / 64, 20.0, 20.0)
 CUTOFF = 5.0
 SPREAD = 2.0 * math.sqrt(math.log2(math.e))
+GAP = 4.5 / 15
+SHRINK = math.exp(-8.0 * GAP * GAP)
+GROUP = 4
 CENTERS = [0.5 + 4.5 * b / 15 for b in range(BASIS)]
 COS_QUARTER = [(-1.0) ** n * (math.pi / 2) ** (2 * n) / math.factorial(2 * n) for n in range(8)]
 SIN_HALF = [(-1.0) ** n * math.pi ** (2 * n + 1) / math.factorial(2 * n + 1) for n in range(8)]
@@ -72,7 +75,7 @@
     rw_ref, mw_ref, cwt_ref, sc_ref, in_sem,
     wpad, wcol, kb, ppad, pcol, tpad, cos_ref, sin_ref, ch_ref, cl_ref, sh_ref, sl_ref,
     ssh_ref, ssl_ref, sch_ref, scl_ref, idx_ref, bit_ref, word_ref,
-    weight_ref, scaled_ref, m_ref, ml_ref, g_ref, outf, outp, gf, gp,
+    mask_t, mask_ref, weight_ref, near_ref, ratio_ref, m_ref, ml_ref, g_ref, graw, gmeta,
     xpos, qall, tq, fsend, frecv, cg_ref, cgs, cgr,
     wave32, sz, rz, res, sg, pk, rz3, xb3, res3,
     rounds, gsend, grecv, psend, precv, qsend, qrecv, fsem, frsem, csend, crecv,
@@ -97,11 +100,18 @@
     def xpeer(off):
         return lax.rem(xi + off, NX) * NZ + zi
 
+    around = [zi] + [lax.rem(zi + off, NZ) for off in range(1, NZ)]
+
     def zat(off):
-        return lax.rem(zi + off, NZ)
+        return around[off % NZ]
 
     def far_first(step):
-        return NZ // 2 + (1 - 2 * lax.rem(step, 2)) * lax.div(step + 1, 2)
+        return NZ // 2 + (1 - 2 * (step % 2)) * ((step + 1) // 2)
+
+    def each(body, carry):
+        for step in range(NZ - 1):
+            carry = body(step, carry)
+        return carry
 
     def zpeer(off):
         return xi * NZ + zat(off)
@@ -133,49 +143,41 @@
             device_id={"dom": target}, device_id_type=MESH,
         )
 
-    for copy in fetches:
+    for copy in fetches[:5]:
         copy.wait()
 
+    xpos[0, 0:3, :] = pos_ref[...]
+    xpos[0, 3:6, :] = fref_ref[...]
+    xpos[0, 6:8, :] = ghost_ref[...].astype(f32)
+
+    pl.semaphore_wait(barrier, NX - 1 + 4)
+
+    ghost_copies = []
+    for slot, target in ((0, upper), (1, lower)):
+        ghost_copies.append(
+            remote(xpos.at[0], gmeta.at[slot], gsend.at[2 * slot], grecv.at[2 * slot], target)
+        )
+        ghost_copies.append(
+            remote(feat_ref, graw.at[slot], gsend.at[2 * slot + 1], grecv.at[2 * slot + 1], target)
+        )
+
+    def x_message(src, dst_ref, send, recv, off):
+        return remote(src, dst_ref.at[off], send.at[off - 1], recv.at[off - 1], xpeer(off))
+
+    for copy in ghost_copies:
+        copy.start()
+    reach_tell(0)
+    pos_copies = {off: x_message(xpos.at[0], xpos, psend, precv, off) for off in (2, 1, 3)}
+    for copy in pos_copies.values():
+        copy.start()
+
+    for copy in fetches[5:]:
+        copy.wait()
     ft32 = feat_ref[...].astype(f32).T
-    ftb = ft32.astype(bf16)
     tpad[...] = jnp.zeros_like(tpad)
     ppad[...] = jnp.zeros_like(ppad)
     ppad[0:3, :] = pos_ref[...]
-    own8 = ppad[0:8, :]
-    pcol[0:ATOM, :] = ppad[...].T
-    p1 = own8.astype(bf16)
-    p2 = (own8 - p1.astype(f32)).astype(bf16)
-    p3 = (own8 - p1.astype(f32) - p2.astype(f32)).astype(bf16)
-    rows_of = iota((ATOM, ATOM), 0)
-    for r in range(2):
-        perm = jnp.where(rows_of == ghost_ref[r : r + 1, :], 1.0, 0.0).astype(bf16)
-        outf[r] = nn(ftb, perm).astype(bf16)
-        outp[r] = nn(p1, perm) + nn(p2, perm) + nn(p3, perm)
-    xpos[0] = own8
-    xpos[0, 3:6, :] = fref_ref[...]
-
-    pl.semaphore_wait(barrier, NX - 1 + 4)
-
-    ghost_copies = []
-    for r, target in ((1, upper), (0, lower)):
-        slot = 1 - r
-        ghost_copies.append(
-            remote(outp.at[r], gp.at[slot], gsend.at[2 * slot], grecv.at[2 * slot], target)
-        )
-        ghost_copies.append(
-            remote(outf.at[r], gf.at[slot], gsend.at[2 * slot + 1], grecv.at[2 * slot + 1], target)
-        )
-
-    def x_message(src, dst_ref, send, recv, off):
-        return remote(src, dst_ref.at[off], send.at[off - 1], recv.at[off - 1], xpeer(off))
-
-    for copy in ghost_copies:
-        copy.start()
-    pos_copies = {off: x_message(xpos.at[0], xpos, psend, precv, off) for off in (2, 1, 3)}
-    for copy in pos_copies.values():
-        copy.start()
-
-    reach_tell(0)
+    pcol[...] = ppad[...].T
 
     wave = wave_ref[...].astype(f32)
     wpad[...] = jnp.zeros_like(wpad)
@@ -237,59 +239,78 @@
     reach_learn(0)
     reach_tell(1)
 
-    px, py, pz = (pos_ref[a : a + 1, :] for a in range(3))
-    shifts = iota((32, ATOM), 0)
-
-    def edge_block(step, carry):
+    def mask_step(step, carry):
+        bits = lax.shift_right_logical(
+            jnp.broadcast_to(word_ref[pl.ds(step, 1), :], (32, ATOM)), iota((32, ATOM), 0)
+        ) & 1
         rows = pl.ds(pl.multiple_of(step * 32, 32), 32)
-        cols = pcol[rows, :]
-        dist2 = jnp.zeros((32, ATOM), f32)
-        for a, own in enumerate((px, py, pz)):
-            delta = cols[:, a : a + 1] - own
-            delta = delta - SIDES[a] * jnp.floor(delta * (1.0 / SIDES[a]) + 0.5)
-            dist2 = dist2 + delta * delta
-        dist = jnp.sqrt(dist2)
-        part = jnp.minimum(dist, CUTOFF) * (1.0 / CUTOFF)
-        fade = poly(COS_QUARTER, part * part)
-        mask = lax.shift_right_logical(
-            jnp.broadcast_to(word_ref[pl.ds(step, 1), :], (32, ATOM)), shifts
-        ) & 1
-        weight_ref[rows, :] = fade * fade * mask.astype(f32)
-        scaled_ref[rows, :] = dist * SPREAD
+        mask_t[rows, :] = bits.astype(f32)
         return carry
 
-    def edge_sums(block, feats):
-        for b in range(BASIS):
+    lax.fori_loop(0, TABLE // 32, mask_step, 0)
+    for block in range(3):
+        mask_ref[block] = mask_t[block * ATOM : (block + 1) * ATOM, :].T
+
+    def edge_sums(block, others, feats):
+        def edge_block(step, carry):
+            rows = pl.ds(pl.multiple_of(step * 32, 32), 32)
+            cols = pcol[rows, :]
+            dist2 = jnp.zeros((32, ATOM), f32)
+            for a in range(3):
+                delta = others[a : a + 1, :] - cols[:, a : a + 1]
+                delta = delta - SIDES[a] * jnp.floor(delta * (1.0 / SIDES[a]) + 0.5)
+                dist2 = dist2 + delta * delta
+            dist = jnp.sqrt(dist2)
+            near = jnp.minimum(dist, CUTOFF)
+            part = near * (1.0 / CUTOFF)
+            fade = poly(COS_QUARTER, part * part)
+            fade = jnp.where(dist < CUTOFF, fade * fade, 0.0)
+            weight_ref[block, rows, :] = fade * mask_ref[block, rows, :]
+            near_ref[block, rows, :] = near * SPREAD
+            ratio_ref[block, rows, :] = jnp.exp((8.0 * GAP) * (near - CENTERS[0]) - 4.0 * GAP * GAP)
+            return carry
+
+        lax.fori_loop(0, ATOM // 32, edge_block, 0)
+        for first in range(0, BASIS, GROUP):
             for start in range(0, ATOM, 32):
-                at = pl.ds(block * ATOM + start, 32)
-                away = scaled_ref[at, :] - SPREAD * CENTERS[b]
-                basis = jnp.exp2(-(away * away)).astype(bf16).astype(f32)
-                high, low = split(basis * weight_ref[at, :])
-                m_ref[b, start : start + 32, :] = high
-                ml_ref[b, start : start + 32, :] = low
-            fresh = nn(feats, m_ref[b]) + nn(feats, ml_ref[b])
-            g_ref[b] = fresh if block == 0 else g_ref[b] + fresh
-
-    lax.fori_loop(0, ATOM // 32, edge_block, 0)
-    edge_sums(0, ftb)
+                at = slice(start, start + 32)
+                away = near_ref[block, at, :] - SPREAD * CENTERS[first]
+                weight = weight_ref[block, at, :]
+                ratio = ratio_ref[block, at, :] * SHRINK**first
+                basis = jnp.exp2(-(away * away))
+                for b in range(first, first + GROUP):
+                    high, low = split(basis.astype(bf16).astype(f32) * weight)
+                    m_ref[b, at, :] = high
+                    ml_ref[b, at, :] = low
+                    if b + 1 < first + GROUP:
+                        basis = basis * ratio
+                        ratio = ratio * SHRINK
+            for b in range(first, first + GROUP):
+                fresh = nn(m_ref[b], feats) + nn(ml_ref[b], feats)
+                g_ref[b] = fresh if block == 0 else g_ref[b] + fresh
+
+    edge_sums(0, pos_ref[...], feat_ref[...])
     reach_learn(1)
     reach_tell(2)
 
     for copy in ghost_copies:
         copy.wait_recv()
+    rows_of = iota((ATOM, ATOM), 0).astype(f32)
     for slot in range(2):
-        ppad[0:8, :] = gp[slot]
-        pcol[(1 + slot) * ATOM : (2 + slot) * ATOM, :] = ppad[...].T
-    lax.fori_loop(ATOM // 32, TABLE // 32, edge_block, 0)
-    edge_sums(1, gf[0])
-    edge_sums(2, gf[1])
-
-    tpad[0:BASIS, :] = rw_ref[...].astype(f32)
-    radial = tpad[...].T
-    messages = jnp.zeros((CHAN, ATOM), f32)
+        meta = gmeta[slot]
+        perm32 = jnp.where(rows_of == meta[7 - slot : 8 - slot, :], 1.0, 0.0)
+        perm = perm32.astype(bf16)
+        p1 = meta.astype(bf16)
+        p2 = (meta - p1.astype(f32)).astype(bf16)
+        p3 = (meta - p1.astype(f32) - p2.astype(f32)).astype(bf16)
+        coords = nn(p1, perm) + nn(p2, perm) + nn(p3, perm)
+        edge_sums(1 + slot, coords, nn(perm32.T.astype(bf16), graw[slot]).astype(bf16))
+
+    radial = rw_ref[...].astype(f32)
+    messages = jnp.zeros((ATOM, CHAN), f32)
     for b in range(BASIS):
-        messages = messages + radial[:, b : b + 1] * g_ref[b]
-    messages_b = messages.astype(bf16)
+        messages = messages + radial[b : b + 1, :] * g_ref[b]
+    messages_b = messages.T.astype(bf16)
     mixT = mw_ref[...].astype(f32).T.astype(bf16)
     before = nn(mixT, messages_b)
     sigmoid = 1.0 / (1.0 + jnp.exp(-before))
@@ -350,7 +371,7 @@
             z_copy(t, far_first(step)).start()
             return carry
 
-        lax.fori_loop(0, NZ - 1, z_start, 0)
+        each(z_start, 0)
 
     def reduce_finish(t):
         def z_take(step, total):
@@ -358,21 +379,21 @@
             z_copy(t, off).wait_recv()
             return total + rz[t, off - 1].astype(f32)
 
-        total = lax.fori_loop(0, NZ - 1, z_take, wave32[z_rows(0), :])
+        total = each(z_take, wave32[z_rows(0), :])
         res[t, z_rows(0), :] = total.astype(bf16)
 
         def a_start(step, carry):
             a_copy(t, far_first(step)).start()
             return carry
 
-        lax.fori_loop(0, NZ - 1, a_start, 0)
+        each(a_start, 0)
 
     def gather_finish(t):
         def a_take(step, carry):
             a_arrival(t, far_first(NZ - 2 - step)).wait_recv()
             return carry
 
-        lax.fori_loop(0, NZ - 1, a_take, 0)
+        each(a_take, 0)
 
     one = jnp.zeros((XROWS, CHAN), f32)
     two = jnp.zeros((XROWS, CHAN), f32)
@@ -479,13 +500,9 @@
     upstream = nn(cw, rounded)
     before_grad = (upstream * slope).astype(bf16)
     pk[0:128, :] = nt(messages_b, before_grad)
-    message_grad = nn(mw_ref[...], before_grad).astype(bf16).astype(f32)
-    lanes = iota((CHAN, CHAN), 1)
-    radial_sum = jnp.zeros((CHAN, CHAN), f32)
+    message_grad = nn(mw_ref[...], before_grad).astype(bf16).astype(f32).T
     for b in range(BASIS):
-        column = jnp.sum(message_grad * g_ref[b], axis=1, keepdims=True)
-        radial_sum = jnp.where(lanes == b, column, radial_sum)
-    pk[192:208, :] = radial_sum.T[0:BASIS, :]
+        pk[192 + b : 193 + b, :] = jnp.sum(message_grad * g_ref[b], axis=0, keepdims=True)
 
     def p_rows(off):
         return pl.ds(pl.multiple_of(zat(off) * PROWS, PROWS), PROWS)
@@ -519,8 +536,8 @@
         z3_copy(off).wait_recv()
         return total + rz3[off - 1].astype(f32)
 
-    lax.fori_loop(0, NZ - 1, z3_start, 0)
-    xb3[xi] = lax.fori_loop(0, NZ - 1, z3_take, pk[p_rows(0), :])
+    each(z3_start, 0)
+    xb3[xi] = each(z3_take, pk[p_rows(0), :])
     for off in (2, 1, 3):
         x3_copy(off).start()
     for off in (1, 3, 2):
@@ -535,8 +552,8 @@
         a3_arrival(far_first(NZ - 2 - step)).wait_recv()
         return carry
 
-    lax.fori_loop(0, NZ - 1, a3_start, 0)
-    lax.fori_loop(0, NZ - 1, a3_take, 0)
+    each(a3_start, 0)
+    each(a3_take, 0)
 
     total_ref[...] = res3[...]
 
@@ -556,7 +573,8 @@
         a3_copy(off).wait_send()
         return carry
 
-    lax.fori_loop(1, NZ, drain, 0)
+    for off in range(1, NZ):
+        drain(off, 0)
 
 
 def finish(
@@ -597,7 +615,7 @@
         vmem((XROWS, 128), f32),
         vmem((7, XROWS, 128), f32),
         vmem((128, ATOM), f32),
-        vmem((TABLE, 128), f32),
+        vmem((ATOM, 128), f32),
         vmem((128, 128), f32),
         *[vmem((NX, XROWS, ATOM), f32)] * 2,
         *[vmem((NX, XROWS, ATOM), bf16)] * 8,
@@ -605,13 +623,11 @@
         vmem((SLOTS, ATOM), jnp.int32),
         vmem((TABLE // 32, ATOM), jnp.int32),
         vmem((TABLE, ATOM), f32),
-        vmem((TABLE, ATOM), f32),
+        *[vmem((3, ATOM, ATOM), f32)] * 4,
         vmem((BASIS, ATOM, ATOM), bf16),
         vmem((BASIS, ATOM, ATOM), bf16),
-        vmem((BASIS, CHAN, ATOM), f32),
-        vmem((2, CHAN, ATOM), bf16),
-        vmem((2, 8, ATOM), f32),
-        vmem((2, CHAN, ATOM), bf16),
+        vmem((BASIS, ATOM, CHAN), f32),
+        vmem((2, ATOM, CHAN), bf16),
         vmem((2, 8, ATOM), f32),
         vmem((NX, 8, ATOM), f32),
         vmem((NX, CHAN, ATOM), bf16),

time: 89.1 us -> 89.3 us (level)
  no operation moved by 1% of the time
where the time goes in v4:
time: 89.3 us; the launch traced here: 89.1 us
  Pallas kernels  88.4 us (99%)
    pallas_call x1, Pallas kernels, on_device(): pl.pallas_call(kernel, out_shape=(jax.ShapeDtypeStruct((3, ATOM), f32), j...  86.8 us

profile of v4, /device:TPU:8, one launch (start us, length us, event | category | flops | bytes accessed | tf_op | source)
XLA Modules:
  0.0 89.1 jit_solution(41397249433023325)
XLA Ops:
  0.6 86.8 %step.1 = (f32[3,256]{1,0:T(4,128)}, bf16[256,128]{1,0:T(8,128)(2,1)}) custom-call(bf16[256,128]{1,0:T(8,128)(2,1)} %feat_in.1, f32[3,256]{1,0:T(4,128)} %pos_in.1, s32[64,256]{1,0:T(8,128)} %bitcast.5, s32[1,256]{1,0:T(1,128)} %bitcast.7, s32[2,256]{1,0:T(2,128)} %ghost_in.1, s32[1,256]{1,0:T(1,128)} %bitcast.8, s32[3,1024]{1,0:T(4,128)} %wave_in.1, ...), custom_call_target="tpu_custom_call" | custom-call | tf_op jit(solution)/shard_map/step/pallas_call | solution.py:662
  87.5 1.6 %finish.1 = (f32[3,256]{1,0:T(4,128)}, f32[16,128]{1,0:T(8,128)}, f32[128,128]{1,0:T(8,128)}, f32[64,128]{1,0:T(8,128)}, f32[6,64]{1,0:T(8,128)}) custom-call(f32[3,256]{1,0:T(4,128)} %get-tuple-element.12.raw_ref, bf16[256,128]{1,0:T(8,128)(2,1)} %get-tuple-element.13.total_ref), custom_call_target="tpu_custom_call" | custom-call | tf_op jit(solution)/shard_map/finish/pallas_call | solution.py:689
